TPU v7x, 512 devices: a whole 4x4x16 slice. The times are simulated.
512 devices in a mesh: ka: 16 (over y, z_hi), row: 4 (over x), col: 8 (over z_lo, core).
Axes of the slice: x: 4, y: 4, z: 16 (z_hi: 4, z_lo: 4; z = z_hi * 4 + z_lo), core: 2. Of those that a mesh axis runs over, the one named last changes fastest.
Arguments:
- exciton: bfloat16 [16, 4, 128, 128], P('ka'), may hold values from -6 to 6
- orb_cond: bfloat16 [16, 128, 2048], P('ka', None, 'row'), may hold values from -0.5 to 0.5
- orb_val: bfloat16 [16, 128, 2048], P('ka', None, 'col'), may hold values from -0.5 to 0.5
- screened: bfloat16 [16, 2048, 2048], P(None, 'row', 'col'), may hold values from -1.5 to 1.5
- q_table: int32 [16, 16], replicated, may hold values from 0 to 15, as said below
Outputs:
- applied: float32 [16, 4, 128, 128], P('ka', None, 'col')
Inputs may be any that keep to these rules, and one draw needn't show every extreme that they name: q_table is the difference table of the k-points of a cyclic grid of 16 points under a relabeling of points and of differences: every row and every column holds each of 0 to 15 once.
All inputs are finite; a program needn't handle non-finite values.
Results may differ from a plain program's by a relative error of at most 0.019.
Values may be sent and summed in bfloat16 or wider, within the bound.
A program may use at most 64 MiB of HBM per device.

v0:
```python
import math

import jax
import jax.numpy as jnp
from jax import lax
from jax.sharding import PartitionSpec as P

NV = 128
NC = 128
NMU = 2048


def split_up(x, dim, devices):
    before, after = (x.shape[:dim], x.shape[dim + 1 :])
    return jnp.moveaxis(x.reshape(*before, devices, -1, *after), dim, 0)


def summed_on_arrival(x, axis, dim):
    blocks = split_up(x, dim, lax.axis_size(axis))
    arrived = lax.all_to_all(blocks, axis, split_axis=0, concat_axis=0, tiled=True)
    return arrived.astype(jnp.float32).sum(axis=0)


def copy_for_each(x, axis):
    devices = lax.axis_size(axis)
    return lax.all_to_all(jnp.broadcast_to(x[None], (devices, *x.shape)), axis, 0, 0, tiled=True)


def of_everyone(x, axis):
    return copy_for_each(x, axis).astype(jnp.float32).sum(axis=0)


def local(exciton, orb_cond, orb_val, screened, q_table):
    local_count = exciton.shape[0]
    own_points = lax.axis_index("ka") * local_count + jnp.arange(local_count, dtype=jnp.int32)
    q_columns = jnp.take(q_table, own_points, axis=1)
    panels = jnp.einsum(
        "kbvc,kcm->kbvm", exciton, orb_cond, preferred_element_type=jnp.float32
    ).astype(jnp.bfloat16)
    start_sum = jnp.zeros(
        (local_count, exciton.shape[1], orb_cond.shape[2], orb_val.shape[2]), jnp.float32
    )

    def weigh_pairs(running, pair_block, position):
        indices = lax.dynamic_index_in_dim(q_columns, position, 0, keepdims=False)
        weights = jnp.take(screened, indices, axis=0).astype(jnp.float32)
        return running + weights[:, None] * pair_block[None].astype(jnp.float32)

    portion = (
        lax.all_gather(panels, "ka", axis=0, tiled=True),
        lax.all_gather(orb_val, "ka", axis=0, tiled=True),
    )

    def one_point(entry_index, inner_sum):
        panel_rows = lax.dynamic_index_in_dim(portion[0], entry_index, 0, keepdims=False)
        valence = lax.dynamic_index_in_dim(portion[1], entry_index, 0, keepdims=False)
        pair_block = jnp.einsum(
            "bvm,vn->bmn", panel_rows, valence, preferred_element_type=jnp.float32
        ).astype(jnp.bfloat16)
        return weigh_pairs(inner_sum, pair_block, entry_index)

    direct = lax.fori_loop(0, portion[0].shape[0], one_point, start_sum)
    direct = direct.astype(jnp.bfloat16)
    half_sums = jnp.einsum(
        "kbmn,kvn->kbmv", direct, orb_val, preferred_element_type=jnp.float32
    ).astype(jnp.bfloat16)
    factor = math.sqrt(NV * NC) / NMU
    partial_value = (
        jnp.einsum("kcm,kbmv->kbvc", orb_cond, half_sums, preferred_element_type=jnp.float32)
        * factor
    )
    shares = summed_on_arrival(partial_value.astype(jnp.bfloat16), "col", 2)
    result = of_everyone(shares.astype(jnp.bfloat16), "row").astype(jnp.float32)
    return result


def solution(mesh):
    placed = (
        P("ka", None, None, None),
        P("ka", None, "row"),
        P("ka", None, "col"),
        P(None, "row", "col"),
        P(),
    )
    return jax.shard_map(
        local, mesh=mesh, in_specs=placed, out_specs=P("ka", None, "col", None), check_vma=False
    )
```

profile of v0, /device:TPU:8, one launch (start us, length us, event | category | flops | bytes accessed | tf_op | source)
XLA Modules:
  0.0 422.1 jit_solution(8037367269032499573)
XLA Ops:
  7.4 2.0 convolution_convert_fusion.2
  10.3 81.8 %all-gather.4.cloned.1.call-done = bf16[16,128,256]{2,1,0:T(8,128)(2,1)} async-done(((bf16[1,128,256]{2,1,0:T(8,128)(2,1)}), bf16[16,128,256]{2,1,0:T(8,128)(2,1)}) %all-gather.4.cloned.1.call-update) | async-done | bytes 1048592 | tf_op jit(solution)/shard_map/all_gather | solution.py:51
  92.1 215.3 %all-gather.6.cloned.1.call-done = bf16[64,128,512]{2,1,0:T(8,128)(2,1)} async-done(((bf16[4,128,512]{2,1,0:T(8,128)(2,1)}), bf16[64,128,512]{2,1,0:T(8,128)(2,1)}) %all-gather.6.cloned.1.call-update) | async-done | bytes 8388624 | tf_op jit(solution)/shard_map/all_gather | solution.py:50
  307.4 86.6 %while.16 = (s32[]{:T(128)}, f32[1,4,512,256]{3,2,1,0:T(8,128)S(1)}, s32[16,1]{0,1:T(1,128)S(1)}, bf16[16,512,256]{2,1,0:T(8,128)(2,1)}, bf16[16,4,128,512]{3,2,...) while((s32[]{:T(128)}, ...), condition=%wide.region_1.2_spmd.clone, body=%wide.region_0.1_spmd.clone.sunk | while | flops 137101312 | bytes 6096063 | solution.py:62
  309.9 1.0 bitcast_convert_fusion.2
  310.9 1.9 bitcast_add_fusion.2
  315.3 1.0 bitcast_convert_fusion.2
  316.3 1.9 bitcast_add_fusion.2
  321.7 1.9 bitcast_add_fusion.2
  326.2 1.0 bitcast_convert_fusion.2
  327.2 1.9 bitcast_add_fusion.2
  331.6 1.0 bitcast_convert_fusion.2
  332.6 1.9 bitcast_add_fusion.2
  337.0 1.0 bitcast_convert_fusion.2
  338.0 1.9 bitcast_add_fusion.2
  342.4 1.0 bitcast_convert_fusion.2
  343.4 1.9 bitcast_add_fusion.2
  348.8 1.9 bitcast_add_fusion.2
  354.2 1.9 bitcast_add_fusion.2
  358.7 1.0 bitcast_convert_fusion.2
  359.7 1.9 bitcast_add_fusion.2
  364.1 1.0 bitcast_convert_fusion.2
  365.1 1.9 bitcast_add_fusion.2
  369.5 1.0 bitcast_convert_fusion.2
  370.5 1.9 bitcast_add_fusion.2
  374.9 1.0 bitcast_convert_fusion.2
  375.9 1.9 bitcast_add_fusion.2
  381.3 1.9 bitcast_add_fusion.2
  386.7 1.9 bitcast_add_fusion.2
  392.1 1.9 bitcast_add_fusion.2
  395.0 10.0 %all_to_all.10 = bf16[8,1,4,16,128]{4,3,2,1,0:T(8,128)(2,1)S(1)} all-to-all(bf16[8,1,4,16,128]{4,3,2,1,0:T(8,128)(2,1)S(1)} %bitcast.59), channel_id=1, replica_groups=mesh['ka'=16,'row'=4,'col'=8] {'col'}, dimensions={0} | all-to-all | bytes 262144 | tf_op jit(solution)/shard_map/all_to_all | solution.py:20
  405.0 9.7 %all_to_all.11 = bf16[4,1,4,16,128]{4,3,2,1,0:T(8,128)(2,1)S(1)} all-to-all(bf16[4,1,4,16,128]{4,3,2,1,0:T(8,128)(2,1)S(1)} %broadcast_in_dim.46), channel_id=1, replica_groups=mesh['ka'=16,'row'=4,'col'=8] {'row'}, dimensions={0} | all-to-all | bytes 131072 | tf_op jit(solution)/shard_map/all_to_all | solution.py:26
  (39 shorter events, 18.8 us)
Async XLA Ops:
  6.5 0.9 copy-start
  6.5 85.6 %all-gather.4.cloned.1.call-start = ((), (), s32[]{:S(2)}) async-start(), calls=%async_computation.2 | async-start | bytes 1114112 | tf_op jit(solution)/shard_map/all_gather | solution.py:51
  7.3 300.2 %all-gather.6.cloned.1.call-start = ((), (), s32[]{:S(2)}) async-start(), calls=%async_computation.3 | async-start | bytes 8912896 | tf_op jit(solution)/shard_map/all_gather | solution.py:50
  307.4 86.6 %copy-start.1 = (bf16[1,128,256]{2,1,0:T(8,128)(2,1)S(1)}, bf16[1,128,256]{2,1,0:T(8,128)(2,1)}, u32[]{:S(2)}) copy-start(bf16[1,128,256]{2,1,0:T(8,128)(2,1)} %param.9) | copy-start | bytes 196612
Sparse Core Ops, SparseCore 0:
  10.3 81.7 all-gather.3
  95.1 212.2 all-gather.5
where the time goes:
time: 424 us; the launch traced here: 422 us
  waiting for transfers between devices  298 us (70%)
  matrix products  33.4 us (8%)
  loops' own time  30.6 us (7%)
  blocking collectives  19.7 us (5%)
  other arithmetic  16.5 us (4%)
  between operations  13.5 us (3%)
  local copies, waits for them, and re-layouts  10.5 us (2%)
    all_gather x1, waiting for transfers between devices, local(): lax.all_gather(panels, 'ka', axis=0, tiled=True)  215 us
    all_gather x1, waiting for transfers between devices, local(): lax.all_gather(orb_val, 'ka', axis=0, tiled=True)  81.8 us
    dot_general x16, matrix products, one_point(): jnp.einsum('bvm,vn->bmn', panel_rows, valence, preferred_element_type=jnp...  30.6 us
    another operation x1, loops' own time, local(): direct = lax.fori_loop(0, portion[0].shape[0], one_point, start_sum)  30.6 us
    convert_element_type x16, other arithmetic, weigh_pairs(): weights = jnp.take(screened, indices, axis=0).astype(jnp.float32)  15.9 us
    all_to_all x1, blocking collectives, summed_on_arrival(): lax.all_to_all(blocks, axis, split_axis=0, concat_axis=0, tiled=True)  9.99 us
    all_to_all x1, blocking collectives, copy_for_each(): lax.all_to_all(jnp.broadcast_to(x[None], (devices, *x.shape)), axis, 0, 0...  9.67 us
    dynamic_slice x16, local copies, waits for them, and re-layouts, weigh_pairs(): indices = lax.dynamic_index_in_dim(q_columns, position, 0, keepdims=False)  9.52 us
  transfers between devices with their start and end apart: 2, of which 2 were waited for; matrix products, arithmetic and copies ran while one was open for 1% of the time, Pallas kernels for 0%

commit v1 on v0

v1 whole, which is shorter than its diff:
```python
import functools
import math

import jax
import jax.numpy as jnp
from jax import lax
from jax.experimental import pallas as pl
from jax.experimental.pallas import tpu as pltpu
from jax.sharding import PartitionSpec as P

NZH = 4
MESH = pl.DeviceIdType.MESH
BF16 = jnp.bfloat16
F32 = jnp.float32
NT = (((1,), (1,)), ((), ()))


def kernel(
    sizes, factor, q_ref, ex_hbm, cond_hbm, val_hbm, w_hbm, out_ref,
    ex_v, cond_v, condt, w_v, wf, psend, pb, vb, pairs, direct, hs, c1, tsum, zr, us, fr, xs,
    ld, p1s, p1r, p2s, p2r, pcs, pcr, v1s, v1r, vas, var, vbs, vbr, vcs, vcr, vds, vdr,
    h1s, h1r, h2s, h2r, h3s, h3r, h5s, h5r,
):
    ny, nzh, nx, nzl = sizes
    nka = ny * nzh
    a, r, c = lax.axis_index("ka"), lax.axis_index("row"), lax.axis_index("col")
    y, zh = a // nzh, a % nzh
    zl, co = c // 2, c % 2
    partner = {"col": zl * 2 + 1 - co}

    def ka(d):
        return (a + d) % nka

    def zl_of(d):
        return (zl + d) % nzl

    def y_of(d):
        return (y + d) % ny

    def zh_of(d):
        return (zh + d) % nzh

    def x_of(d):
        return (r + d) % nx

    def send(src, dst, ss, rs, where):
        pltpu.make_async_remote_copy(
            src_ref=src, dst_ref=dst, send_sem=ss, recv_sem=rs, device_id=where, device_id_type=MESH
        ).start()

    def got(ref, rs):
        pltpu.make_async_copy(ref, ref, rs).wait()

    def each(n, body):
        def step(d, carry):
            body(d)
            return carry

        lax.fori_loop(1, n, step, 0)

    load_ex = pltpu.make_async_copy(ex_hbm.at[zl], ex_v, ld.at[0])
    load_cond = pltpu.make_async_copy(cond_hbm, cond_v, ld.at[1])
    load_val = pltpu.make_async_copy(val_hbm.at[r], vb.at[a, r], ld.at[2])
    load_w = pltpu.make_async_copy(w_hbm.at[:, a], w_v, ld.at[3])
    load_val.start()
    load_cond.start()
    load_ex.start()
    load_w.start()

    barrier = pltpu.get_barrier_semaphore()

    def hello(where):
        pl.semaphore_signal(barrier, inc=1, device_id=where, device_id_type=MESH)

    each(nka, lambda d: hello({"ka": ka(d)}))
    each(nzl, lambda d: hello({"col": zl_of(d) * 2 + co}))
    each(nx, lambda d: hello({"row": x_of(d)}))
    hello(partner)

    load_cond.wait()
    load_ex.wait()
    condt[...] = cond_v[...].T
    psend[...] = (
        lax.dot_general(condt[...], ex_v[...], NT, preferred_element_type=F32)
        .astype(BF16)
        .reshape(psend.shape)
    )
    pb[a, zl, co] = psend[a, co]
    load_val.wait()
    pl.semaphore_wait(barrier, nka + nzl + nx - 2)

    def v1(d):
        send(vb.at[a, r], vb.at[a, r], v1s.at[d], v1r.at[d], {"ka": y * nzh + zh_of(d)})

    each(nzh, v1)

    def p1(d):
        send(psend.at[ka(d), co], pb.at[a, zl, co], p1s.at[d], p1r.at[d], {"ka": ka(d)})

    each(nka, p1)

    load_w.wait()
    wf[...] = w_v[...].astype(F32)

    each(nzh, lambda d: got(vb.at[a, r], v1r.at[d]))
    mine = pl.ds(y * nzh, nzh)

    def v2a(d):
        part = vb.at[mine, r, 0]
        send(part, part, vas.at[d], var.at[d], {"ka": y_of(d) * nzh + zh})

    def v2b(d):
        part = vb.at[mine, r, 1]
        send(part, part, vbs.at[d], vbr.at[d], {"row": x_of(d)})

    each(ny, v2a)
    each(nx, v2b)

    each(nka, lambda d: got(pb.at[a, zl, co], p1r.at[d]))

    def p2(d):
        part = pb.at[:, zl, co]
        send(part, part, p2s.at[d], p2r.at[d], {"col": zl_of(d) * 2 + co})

    def pc(d):
        part = pb.at[:, (zl + nzl - d) % nzl, co]
        send(part, part, pcs.at[d], pcr.at[d], partner)

    each(nzl, p2)
    pc(0)

    each(ny, lambda d: got(vb.at[mine, r, 0], var.at[d]))

    def v3a(d):
        part = vb.at[:, r, 0]
        send(part, part, vcs.at[d], vcr.at[d], {"row": x_of(d)})

    each(nx, v3a)
    each(nx, lambda d: got(vb.at[mine, r, 1], vbr.at[d]))

    def v3b(d):
        part = vb.at[mine, :, 1]
        send(part, part, vds.at[d], vdr.at[d], {"ka": y_of(d) * nzh + zh})

    each(ny, v3b)

    def p2_got(d):
        got(pb.at[:, zl, co], p2r.at[d])
        pc(d)

    each(nzl, p2_got)
    got(pb.at[:, zl, co], pcr.at[0])
    each(nzl, lambda d: got(pb.at[:, zl, co], pcr.at[d]))
    each(nx, lambda d: got(vb.at[:, r, 0], vcr.at[d]))
    each(ny, lambda d: got(vb.at[mine, :, 1], vdr.at[d]))

    rows, nv, nnu = nzl * 32, nzl * 32, vb.shape[-1]

    def pair(k, carry):
        panel = pb[k].reshape(rows, nv)
        val = vb[k].reshape(nv, nnu)
        pairs[k] = jnp.dot(panel, val, preferred_element_type=F32).reshape(nzl, 32, nnu)
        return carry

    lax.fori_loop(0, nka, pair, 0)

    kg = min(8, nka)
    lanes = nnu // 128

    def weigh(t, carry):
        g = t // (4 * lanes)
        s = pl.ds(pl.multiple_of(((t // lanes) % 4) * 8, 8), 8)
        l = pl.ds(pl.multiple_of((t % lanes) * 128, 128), 128)
        sums = [[None] * nzl for _ in range(kg)]
        for k2 in range(nka):
            p = [pairs[k2, b, s, l] for b in range(nzl)]
            for i in range(kg):
                w = wf[q_ref[k2, g * kg + i], s, l]
                for b in range(nzl):
                    term = w * p[b]
                    sums[i][b] = term if k2 == 0 else sums[i][b] + term
        for i in range(kg):
            for b in range(nzl):
                direct[g * kg + i, b, s, l] = sums[i][b]
        return carry

    lax.fori_loop(0, (nka // kg) * 4 * lanes, weigh, 0)

    def half(k, carry):
        d = direct[k].reshape(rows, nnu).astype(BF16)
        val = vb[k].reshape(nv, nnu)
        h = lax.dot_general(val, d, NT, preferred_element_type=F32)
        hs[k] = h.astype(BF16).reshape(nzl, 2, 16, rows)
        return carry

    lax.fori_loop(0, nka, half, 0)

    send(hs.at[:, :, 1 - co], c1, h1s.at[0], h1r.at[0], partner)
    got(c1, h1r.at[0])

    def add_core(k, carry):
        tsum[:, k] = (hs[k, :, co].astype(F32) + c1[k].astype(F32)).astype(BF16)
        return carry

    lax.fori_loop(0, nka, add_core, 0)

    def h2(d):
        send(tsum.at[zl_of(d)], zr.at[d], h2s.at[d], h2r.at[d], {"col": zl_of(d) * 2 + co})

    each(nzl, h2)
    each(nzl, lambda d: got(zr.at[d], h2r.at[d]))

    def add_zl(k, carry):
        total = tsum[zl, k].astype(F32)
        for d in range(1, nzl):
            total = total + zr[d, k].astype(F32)
        us[k] = total.astype(BF16)
        return carry

    lax.fori_loop(0, nka, add_zl, 0)

    def h3(d):
        send(us.at[ka(d)], fr.at[a], h3s.at[d], h3r.at[d], {"ka": ka(d)})

    each(nka, h3)
    fr[a] = us[a]
    each(nka, lambda d: got(fr.at[a], h3r.at[d]))

    lane_b = lax.broadcasted_iota(jnp.int32, (16, rows), 1) // 32

    def last(k, total):
        f = fr[k].astype(F32)
        lhs = jnp.concatenate(
            [jnp.where(lane_b == b, f, 0.0) for b in range(nzl)], axis=0
        ).astype(BF16)
        ct = condt[pl.ds(pl.multiple_of(k * 32, 32), 32), :]
        rhs = jnp.concatenate([ct] * nzl, axis=0)
        return total + jnp.dot(lhs, rhs, preferred_element_type=F32)

    total = lax.fori_loop(0, nka, last, jnp.zeros((nzl * 16, condt.shape[1]), F32))
    xs[r] = total.astype(BF16)

    def h5(d):
        send(xs.at[r], xs.at[r], h5s.at[d], h5r.at[d], {"row": x_of(d)})

    each(nx, h5)
    each(nx, lambda d: got(xs.at[r], h5r.at[d]))
    result = xs[0].astype(F32)
    for i in range(1, nx):
        result = result + xs[i].astype(F32)
    out_ref[...] = (result * factor).reshape(out_ref.shape)

    each(nzh, lambda d: got(vb.at[a, r], v1s.at[d]))
    each(nka, lambda d: got(pb.at[a, zl, co], p1s.at[d]))
    each(ny, lambda d: got(vb.at[mine, r, 0], vas.at[d]))
    each(nx, lambda d: got(vb.at[mine, r, 1], vbs.at[d]))
    each(nzl, lambda d: got(pb.at[:, zl, co], p2s.at[d]))
    got(pb.at[:, zl, co], pcs.at[0])
    each(nzl, lambda d: got(pb.at[:, zl, co], pcs.at[d]))
    each(nx, lambda d: got(vb.at[:, r, 0], vcs.at[d]))
    each(ny, lambda d: got(vb.at[mine, :, 1], vds.at[d]))
    got(c1, h1s.at[0])
    each(nzl, lambda d: got(zr.at[d], h2s.at[d]))
    each(nka, lambda d: got(fr.at[a], h3s.at[d]))
    each(nx, lambda d: got(xs.at[r], h5s.at[d]))


def local(sizes, factor, exciton, orb_cond, orb_val, screened, q_table):
    ny, nzh, nx, nzl = sizes
    nka = ny * nzh
    nc = exciton.shape[-1]
    nv = nzl * 32
    rows = nzl * 32
    mu = nka * 32
    nnu = orb_val.shape[-1]
    any_space = pl.BlockSpec(memory_space=pl.ANY)
    dma = lambda n: pltpu.SemaphoreType.DMA((n,))
    vm = pltpu.VMEM
    out = pl.pallas_call(
        functools.partial(kernel, sizes, factor),
        name="isdf_direct",
        out_shape=jax.ShapeDtypeStruct((nzl, 16, nc), F32),
        in_specs=[pl.BlockSpec(memory_space=pltpu.SMEM)] + [any_space] * 4,
        out_specs=pl.BlockSpec(memory_space=pltpu.VMEM),
        scratch_shapes=[
            vm((nv, nc), BF16),
            vm((nc, mu), BF16),
            vm((mu, nc), BF16),
            vm((nka, 32, nnu), BF16),
            vm((nka, 32, nnu), F32),
            vm((nka, 2, 16, nv), BF16),
            vm((nka, nzl, 2, 16, nv), BF16),
            vm((nka, nx, 2, 16, nnu), BF16),
            vm((nka, nzl, 32, nnu), F32),
            vm((nka, nzl, 32, nnu), F32),
            vm((nka, nzl, 2, 16, rows), BF16),
            vm((nka, nzl, 16, rows), BF16),
            vm((nzl, nka, 16, rows), BF16),
            vm((nzl, nka, 16, rows), BF16),
            vm((nka, 16, rows), BF16),
            vm((nka, 16, rows), BF16),
            vm((nx, nzl * 16, nc), BF16),
            dma(4),
            dma(nka), dma(nka),
            dma(nzl), dma(nzl), dma(nzl), dma(nzl),
            dma(nzh), dma(nzh),
            dma(ny), dma(ny), dma(nx), dma(nx),
            dma(nx), dma(nx), dma(ny), dma(ny),
            dma(1), dma(1), dma(nzl), dma(nzl),
            dma(nka), dma(nka), dma(nx), dma(nx),
        ],
        compiler_params=pltpu.CompilerParams(
            collective_id=0, has_side_effects=True, vmem_limit_bytes=56 * 1024 * 1024
        ),
    )(
        q_table,
        exciton[0],
        orb_cond[0],
        orb_val.reshape(nx, 2, 16, nnu),
        screened.reshape(nka, nka, 32, nnu),
    )
    return out[None]


def build(mesh, nzh, factor):
    shape = mesh.shape
    sizes = (shape["ka"] // nzh, nzh, shape["row"], shape["col"] // 2)
    placed = (
        P("ka", None, None, None),
        P("ka", None, "row"),
        P("ka", None, "col"),
        P(None, "row", "col"),
        P(),
    )
    return jax.shard_map(
        functools.partial(local, sizes, factor),
        mesh=mesh, in_specs=placed, out_specs=P("ka", None, "col", None), check_vma=False,
    )


def solution(mesh):
    return build(mesh, NZH, math.sqrt(128 * 128) / 2048)
```

time: 424 us -> 75 us (0.18)
  the two profiles are of different devices: /device:TPU:8 before, /device:TPU:32 now
where the time goes in v1:
time: 75 us; the launch traced here: 74.7 us
  Pallas kernels  73.3 us (98%)
  local copies, waits for them, and re-layouts  1.38 us (2%)
    pallas_call x1, Pallas kernels, local(): pl.pallas_call(functools.partial(kernel, sizes, factor), name='isdf_direc...  73.3 us

profile of v1, /device:TPU:32, one launch (start us, length us, event | category | flops | bytes accessed | tf_op | source)
XLA Modules:
  0.0 74.7 jit_solution(13390022701953674810)
XLA Ops:
  0.0 73.3 %isdf_direct.1 = f32[4,16,128]{2,1,0:T(8,128)} custom-call(s32[16,16]{1,0:T(8,128)} %q_ref.1, bf16[4,128,128]{2,1,0:T(8,128)(2,1)} %bitcast.7, bf16[128,512]{1,0:T(8,128)(2,1)} %bitcast.8, bf16[4,2,16,256]{3,2,1,0:T(8,128)(2,1)} %bitcast.9, bf16[16,16,32,256]{3,2,1,0:T(8,128)(2,1)} %bitcast.5), custom_call_target="tpu_custom_call" | custom-call | tf_op jit(solution)/shard_map/isdf_direct/pallas_call | solution.py:279
  73.3 1.4 %copy.7 = f32[1,4,16,128]{3,2,1,0:T(8,128)} copy(f32[1,4,16,128]{3,2,1,0:T(8,128)} %bitcast.6) | data formatting | bytes 65536

commit v2 on v0

v2 whole, which is shorter than its diff:
```python
import functools
import math

import jax
import jax.numpy as jnp
from jax import lax
from jax.experimental import pallas as pl
from jax.experimental.pallas import tpu as pltpu
from jax.sharding import PartitionSpec as P

NZH = 4
MESH = pl.DeviceIdType.MESH
BF16 = jnp.bfloat16
F32 = jnp.float32
NT = (((1,), (1,)), ((), ()))


def kernel(
    sizes, factor, q_ref, ex_hbm, cond_hbm, val_hbm, w_hbm, out_ref,
    ex_v, cond_v, condt, ct4, w_v, wf, psend, pb, vb, pairs, direct, hs, c1, tsum, zr, us, fr, xs,
    ld, p1s, p1r, p2s, p2r, pcs, pcr, v1s, v1r, vas, var, vbs, vbr, vcs, vcr, vds, vdr,
    h1s, h1r, h2s, h2r, h3s, h3r, h5s, h5r,
):
    ny, nzh, nx, nzl = sizes
    nka = ny * nzh
    rows, nv, nnu, nc = nzl * 32, nzl * 32, vb.shape[-1], condt.shape[-1]
    a, r, c = lax.axis_index("ka"), lax.axis_index("row"), lax.axis_index("col")
    y, zh = a // nzh, a % nzh
    zl, co = c // 2, c % 2
    partner = {"col": zl * 2 + 1 - co}
    near = sorted(range(nzh), key=lambda d: min(d, nzh - d))

    def at_ka(dy, dz):
        return {"ka": ((y + dy) % ny) * nzh + (zh + dz) % nzh}

    def at_zl(d):
        return {"col": ((zl + d) % nzl) * 2 + co}

    def at_row(d):
        return {"row": (r + d) % nx}

    def zof(d):
        return (zh + d) % nzh

    def send(src, dst, ss, rs, where):
        pltpu.make_async_remote_copy(
            src_ref=src, dst_ref=dst, send_sem=ss, recv_sem=rs, device_id=where, device_id_type=MESH
        ).start()

    def got(ref, rs):
        pltpu.make_async_copy(ref, ref, rs).wait()

    def each(lo, hi, body):
        def step(d, carry):
            body(d)
            return carry

        if hi > lo:
            lax.fori_loop(lo, hi, step, 0)

    load_ex = pltpu.make_async_copy(ex_hbm.at[zl], ex_v, ld.at[0])
    load_cond = pltpu.make_async_copy(cond_hbm, cond_v, ld.at[1])
    load_val = pltpu.make_async_copy(val_hbm.at[r], vb.at[zh, y, r], ld.at[2])
    load_w = pltpu.make_async_copy(w_hbm.at[:, a], w_v, ld.at[3])
    load_cond.start()
    load_ex.start()
    load_val.start()

    barrier = pltpu.get_barrier_semaphore()

    def hello(where):
        pl.semaphore_signal(barrier, inc=1, device_id=where, device_id_type=MESH)

    for dz in reversed(near):
        each(1 if dz == 0 else 0, ny, lambda dy: hello(at_ka(dy, dz)))
    each(1, nzl, lambda d: hello(at_zl(d)))
    each(1, nx, lambda d: hello(at_row(d)))
    hello(partner)
    load_w.start()

    load_cond.wait()
    condt[...] = cond_v[...].T.reshape(condt.shape)
    load_ex.wait()
    half_cond = condt[:, co].reshape(nka * 16, nc)
    psend[...] = (
        lax.dot_general(half_cond, ex_v[...], NT, preferred_element_type=F32)
        .astype(BF16)
        .reshape(psend.shape)
    )
    pb[zh, y, zl, co] = psend[a]
    load_val.wait()
    pl.semaphore_wait(barrier, nka + nzl + nx - 2)

    for dz in reversed(near):
        if dz:
            part = vb.at[zh, y, r]
            send(part, part, v1s.at[dz], v1r.at[(nzh - dz) % nzh], at_ka(0, dz))

    for dz in reversed(near):

        def p1(dy, dz=dz):
            to = ((y + dy) % ny) * nzh + zof(dz)
            send(
                psend.at[to], pb.at[zh, y, zl, co], p1s.at[dz, dy], p1r.at[(nzh - dz) % nzh],
                at_ka(dy, dz),
            )

        each(1 if dz == 0 else 0, ny, p1)

    load_w.wait()
    wf[...] = w_v[...].astype(F32)
    for k in range(nka):
        for b in range(nzl):
            ct4[k % nzh, k // nzh, b] = condt[k].reshape(32, nc)

    def first(d):
        zs = zof(d)
        if d:
            got(vb.at[zs, y, r], v1r.at[d])

        def v2a(e):
            part = vb.at[zs, y, r, 0]
            send(part, part, vas.at[d, e], var.at[d], at_ka(e, 0))

        def v2b(e):
            part = vb.at[zs, y, r, 1]
            send(part, part, vbs.at[d, e], vbr.at[d], at_row(e))

        each(1, ny, v2a)
        each(1, nx, v2b)
        have = ny if d else ny - 1
        if have:
            got(pb.at[zs, 0:have, zl, co], p1r.at[d])

        def p2(e):
            part = pb.at[zs, :, zl, co]
            send(part, part, p2s.at[d, e], p2r.at[d], at_zl(e))

        each(1, nzl, p2)

    def second(d):
        zs = zof(d)
        if ny > 1:
            got(vb.at[zs, 0 : ny - 1, r, 0], var.at[d])

        def v3a(e):
            part = vb.at[zs, :, r, 0]
            send(part, part, vcs.at[d, e], vcr.at[d], at_row(e))

        each(1, nx, v3a)
        if nx > 1:
            got(vb.at[zs, y, 0 : nx - 1, 1], vbr.at[d])

        def v3b(e):
            part = vb.at[zs, y, :, 1]
            send(part, part, vds.at[d, e], vdr.at[d], at_ka(e, 0))

        each(1, ny, v3b)
        if nzl > 1:
            got(pb.at[zs, :, 0 : nzl - 1, co], p2r.at[d])
        part = pb.at[zs, :, :, co]
        send(part, part, pcs.at[d], pcr.at[d], partner)

    def third(d):
        zs = zof(d)
        got(pb.at[zs, :, :, co], pcr.at[d])
        if nx > 1:
            got(vb.at[zs, :, 0 : nx - 1, 0], vcr.at[d])
        if ny > 1:
            got(vb.at[zs, 0 : ny - 1, :, 1], vdr.at[d])

        def pair(i, carry):
            panel = pb[zs, i].reshape(rows, nv)
            val = vb[zs, i].reshape(nv, nnu)
            pairs[zs, i] = jnp.dot(panel, val, preferred_element_type=F32).reshape(nzl, 32, nnu)
            return carry

        lax.fori_loop(0, ny, pair, 0)

    if nzh == 4:
        plan = (
            (first, 0), (first, 1), (first, 3), (second, 0), (first, 2), (second, 1),
            (second, 3), (third, 0), (second, 2), (third, 1), (third, 3), (third, 2),
        )
    else:
        plan = [(leg, d) for leg in (first, second, third) for d in near]
    for leg, d in plan:
        leg(d)

    lanes = nnu // 128

    def weigh(e):
        zk = zof(e)

        def tile(t, carry):
            s = pl.ds(pl.multiple_of((t // lanes) * 8, 8), 8)
            l = pl.ds(pl.multiple_of((t % lanes) * 128, 128), 128)
            sums = [[None] * nzl for _ in range(ny)]
            for z2 in range(nzh):
                for y2 in range(ny):
                    p = [pairs[z2, y2, b, s, l] for b in range(nzl)]
                    for i in range(ny):
                        w = wf[q_ref[y2 * nzh + z2, i * nzh + zk], s, l]
                        for b in range(nzl):
                            term = w * p[b]
                            sums[i][b] = term if sums[i][b] is None else sums[i][b] + term
            for i in range(ny):
                for b in range(nzl):
                    direct[i, b, s, l] = sums[i][b]
            return carry

        lax.fori_loop(0, 4 * lanes, tile, 0)

        def half(i, carry):
            d = direct[i].reshape(rows, nnu).astype(BF16)
            val = vb[zk, i].reshape(nv, nnu)
            h = lax.dot_general(val, d, NT, preferred_element_type=F32)
            hs[zk, i] = h.astype(BF16).reshape(nzl, 2, 16, rows)
            return carry

        lax.fori_loop(0, ny, half, 0)
        send(hs.at[zk, :, :, 1 - co], c1.at[zk], h1s.at[e], h1r.at[e], partner)

    def over_zl(e):
        zk = zof(e)
        got(c1.at[zk], h1r.at[e])

        def add_core(i, carry):
            tsum[zk, :, i] = (hs[zk, i, :, co].astype(F32) + c1[zk, i].astype(F32)).astype(BF16)
            return carry

        lax.fori_loop(0, ny, add_core, 0)

        def h2(d):
            send(
                tsum.at[zk, (zl + d) % nzl], zr.at[zk, d], h2s.at[e, d], h2r.at[e], at_zl(d)
            )

        each(1, nzl, h2)

    def over_ka(e):
        zk = zof(e)
        if nzl > 1:
            got(zr.at[zk, 0 : nzl - 1], h2r.at[e])

        def add_zl(i, carry):
            total = tsum[zk, zl, i].astype(F32)
            for d in range(1, nzl):
                total = total + zr[zk, d, i].astype(F32)
            us[zk, i] = total.astype(BF16)
            return carry

        lax.fori_loop(0, ny, add_zl, 0)

        def h3(dy):
            send(
                us.at[zk, (y + dy) % ny], fr.at[zh, y], h3s.at[e, dy], h3r.at[(nzh - e) % nzh],
                at_ka(dy, e),
            )

        each(1 if e == 0 else 0, ny, h3)
        if e == 0:
            fr[zh, y] = us[zh, y]

    far = near[::-1]
    for i, e in enumerate(far):
        weigh(e)
        if i:
            over_zl(far[i - 1])
    if nzh > 1:
        over_ka(far[0])
    over_zl(far[-1])
    for e in far[1:] if nzh > 1 else far:
        over_ka(e)

    lane_b = lax.broadcasted_iota(jnp.int32, (16, rows), 1) // 32
    total = jnp.zeros((nzl * 16, nc), F32)
    for d in near:
        have = ny if d else ny - 1
        zs = zof(d)
        if have:
            got(fr.at[zs, 0:have], h3r.at[d])
        for i in range(ny):
            f = fr[zs, i].astype(F32)
            lhs = jnp.concatenate(
                [jnp.where(lane_b == b, f, 0.0) for b in range(nzl)], axis=0
            ).astype(BF16)
            total = total + jnp.dot(
                lhs, ct4[zs, i].reshape(rows, nc), preferred_element_type=F32
            )
    xs[r] = total.astype(BF16)

    def h5(d):
        send(xs.at[r], xs.at[r], h5s.at[d], h5r.at[d], at_row(d))

    each(1, nx, h5)
    each(1, nx, lambda d: got(xs.at[r], h5r.at[d]))
    result = xs[0].astype(F32)
    for i in range(1, nx):
        result = result + xs[i].astype(F32)
    out_ref[...] = (result * factor).reshape(out_ref.shape)

    for d in range(nzh):
        if d:
            got(vb.at[zh, y, r], v1s.at[d])
        lo = 0 if d else 1
        each(lo, ny, lambda e: got(pb.at[zh, y, zl, co], p1s.at[d, e]))
        each(1, ny, lambda e: got(vb.at[zh, y, r, 0], vas.at[d, e]))
        each(1, nx, lambda e: got(vb.at[zh, y, r, 1], vbs.at[d, e]))
        each(1, nzl, lambda e: got(pb.at[zh, :, zl, co], p2s.at[d, e]))
        each(1, nx, lambda e: got(vb.at[zh, :, r, 0], vcs.at[d, e]))
        each(1, ny, lambda e: got(vb.at[zh, y, :, 1], vds.at[d, e]))
        got(pb.at[zh, :, :, co], pcs.at[d])
        got(c1.at[zh], h1s.at[d])
        each(1, nzl, lambda e: got(zr.at[zh, 0], h2s.at[d, e]))
        each(lo, ny, lambda e: got(fr.at[zh, y], h3s.at[d, e]))
    each(1, nx, lambda d: got(xs.at[r], h5s.at[d]))


def local(sizes, factor, exciton, orb_cond, orb_val, screened, q_table):
    ny, nzh, nx, nzl = sizes
    nka = ny * nzh
    nc = exciton.shape[-1]
    nv = nzl * 32
    rows = nzl * 32
    mu = nka * 32
    nnu = orb_val.shape[-1]
    any_space = pl.BlockSpec(memory_space=pl.ANY)
    dma = lambda *n: pltpu.SemaphoreType.DMA(n)
    vm = pltpu.VMEM
    out = pl.pallas_call(
        functools.partial(kernel, sizes, factor),
        name="isdf_direct",
        out_shape=jax.ShapeDtypeStruct((nzl, 16, nc), F32),
        in_specs=[pl.BlockSpec(memory_space=pltpu.SMEM)] + [any_space] * 4,
        out_specs=pl.BlockSpec(memory_space=pltpu.VMEM),
        scratch_shapes=[
            vm((nv, nc), BF16),
            vm((nc, mu), BF16),
            vm((nka, 2, 16, nc), BF16),
            vm((nzh, ny, nzl, 32, nc), BF16),
            vm((nka, 32, nnu), BF16),
            vm((nka, 32, nnu), F32),
            vm((nka, 16, nv), BF16),
            vm((nzh, ny, nzl, 2, 16, nv), BF16),
            vm((nzh, ny, nx, 2, 16, nnu), BF16),
            vm((nzh, ny, nzl, 32, nnu), F32),
            vm((ny, nzl, 32, nnu), F32),
            vm((nzh, ny, nzl, 2, 16, rows), BF16),
            vm((nzh, ny, nzl, 16, rows), BF16),
            vm((nzh, nzl, ny, 16, rows), BF16),
            vm((nzh, nzl, ny, 16, rows), BF16),
            vm((nzh, ny, 16, rows), BF16),
            vm((nzh, ny, 16, rows), BF16),
            vm((nx, nzl * 16, nc), BF16),
            dma(4),
            dma(nzh, ny), dma(nzh),
            dma(nzh, nzl), dma(nzh), dma(nzh), dma(nzh),
            dma(nzh), dma(nzh),
            dma(nzh, ny), dma(nzh), dma(nzh, nx), dma(nzh),
            dma(nzh, nx), dma(nzh), dma(nzh, ny), dma(nzh),
            dma(nzh), dma(nzh), dma(nzh, nzl), dma(nzh),
            dma(nzh, ny), dma(nzh), dma(nx), dma(nx),
        ],
        compiler_params=pltpu.CompilerParams(
            collective_id=0, has_side_effects=True, vmem_limit_bytes=56 * 1024 * 1024
        ),
    )(
        q_table,
        exciton[0],
        orb_cond[0],
        orb_val.reshape(nx, 2, 16, nnu),
        screened.reshape(nka, nka, 32, nnu),
    )
    return out[None]


def build(mesh, nzh, factor):
    shape = mesh.shape
    sizes = (shape["ka"] // nzh, nzh, shape["row"], shape["col"] // 2)
    placed = (
        P("ka", None, None, None),
        P("ka", None, "row"),
        P("ka", None, "col"),
        P(None, "row", "col"),
        P(),
    )
    return jax.shard_map(
        functools.partial(local, sizes, factor),
        mesh=mesh, in_specs=placed, out_specs=P("ka", None, "col", None), check_vma=False,
    )


def solution(mesh):
    return build(mesh, NZH, math.sqrt(128 * 128) / 2048)
```

time: 424 us -> 64.4 us (0.15)
  the two profiles are of different devices: /device:TPU:8 before, /device:TPU:96 now
where the time goes in v2:
time: 64.4 us; the launch traced here: 64.2 us
  Pallas kernels  62.8 us (98%)
  local copies, waits for them, and re-layouts  1.38 us (2%)
    pallas_call x1, Pallas kernels, local(): pl.pallas_call(functools.partial(kernel, sizes, factor), name='isdf_direc...  62.8 us
    unnamed x1, local copies, waits for them, and re-layouts  1.38 us

profile of v2, /device:TPU:96, one launch (start us, length us, event | category | flops | bytes accessed | tf_op | source)
XLA Modules:
  0.0 64.2 jit_solution(18321566820112391523)
XLA Ops:
  0.0 62.8 %isdf_direct.1 = f32[4,16,128]{2,1,0:T(8,128)} custom-call(s32[16,16]{1,0:T(8,128)} %q_ref.1, bf16[4,128,128]{2,1,0:T(8,128)(2,1)} %bitcast.7, bf16[128,512]{1,0:T(8,128)(2,1)} %bitcast.8, bf16[4,2,16,256]{3,2,1,0:T(8,128)(2,1)} %bitcast.9, bf16[16,16,32,256]{3,2,1,0:T(8,128)(2,1)} %bitcast.5), custom_call_target="tpu_custom_call" | custom-call | tf_op jit(solution)/shard_map/isdf_direct/pallas_call | solution.py:331
  62.8 1.4 %copy.7 = f32[1,4,16,128]{3,2,1,0:T(8,128)} copy(f32[1,4,16,128]{3,2,1,0:T(8,128)} %bitcast.6) | data formatting | bytes 65536

commit v3 on v2

--- a/solution.py
+++ b/solution.py
@@ -16,9 +16,9 @@
 
 
 def kernel(
-    sizes, factor, q_ref, ex_hbm, cond_hbm, val_hbm, w_hbm, out_ref,
-    ex_v, cond_v, condt, ct4, w_v, wf, psend, pb, vb, pairs, direct, hs, c1, tsum, zr, us, fr, xs,
-    ld, p1s, p1r, p2s, p2r, pcs, pcr, v1s, v1r, vas, var, vbs, vbr, vcs, vcr, vds, vdr,
+    sizes, factor, q_hbm, ex_hbm, cond_hbm, val_hbm, w_hbm, out_ref,
+    q_ref, ex_v, cond_v, condt, ct4, w_v, wf, psend, prel, pb, vb, pairs, direct, hs, c1, tsum, zr, us, fr, xs,
+    ld, p1s, p1r, prr, pfs, p2s, p2r, pcs, pcr, v1s, v1r, vxr, vfs, vgs, vys, vyr, vas, var, vbs, vbr, vcs, vcr, vds, vdr,
     h1s, h1r, h2s, h2r, h3s, h3r, h5s, h5r,
 ):
     ny, nzh, nx, nzl = sizes
@@ -29,6 +29,9 @@
     zl, co = c // 2, c % 2
     partner = {"col": zl * 2 + 1 - co}
     near = sorted(range(nzh), key=lambda d: min(d, nzh - d))
+    beside = [d for d in near if min(d, nzh - d) < 2]
+    opposite = nzh > 2
+    hy = ny // 2
 
     def at_ka(dy, dz):
         return {"ka": ((y + dy) % ny) * nzh + (zh + dz) % nzh}
@@ -62,6 +65,7 @@
     load_cond = pltpu.make_async_copy(cond_hbm, cond_v, ld.at[1])
     load_val = pltpu.make_async_copy(val_hbm.at[r], vb.at[zh, y, r], ld.at[2])
     load_w = pltpu.make_async_copy(w_hbm.at[:, a], w_v, ld.at[3])
+    load_q = pltpu.make_async_copy(q_hbm, q_ref, ld.at[4])
     load_cond.start()
     load_ex.start()
     load_val.start()
@@ -71,12 +75,19 @@
     def hello(where):
         pl.semaphore_signal(barrier, inc=1, device_id=where, device_id_type=MESH)
 
-    for dz in reversed(near):
+    for dz in reversed(beside):
         each(1 if dz == 0 else 0, ny, lambda dy: hello(at_ka(dy, dz)))
+    if opposite:
+
+        @pl.when(zh < 2)
+        def _():
+            each(0, ny, lambda dy: hello(at_ka(dy, 2)))
+
     each(1, nzl, lambda d: hello(at_zl(d)))
     each(1, nx, lambda d: hello(at_row(d)))
     hello(partner)
     load_w.start()
+    load_q.start()
 
     load_cond.wait()
     condt[...] = cond_v[...].T.reshape(condt.shape)
@@ -89,14 +100,42 @@
     )
     pb[zh, y, zl, co] = psend[a]
     load_val.wait()
-    pl.semaphore_wait(barrier, nka + nzl + nx - 2)
-
-    for dz in reversed(near):
-        if dz:
-            part = vb.at[zh, y, r]
-            send(part, part, v1s.at[dz], v1r.at[(nzh - dz) % nzh], at_ka(0, dz))
-
-    for dz in reversed(near):
+    greeted = ny * len(beside) + nzl + nx - 2
+    if opposite:
+        greeted = greeted + ny * (zh // 2)
+    pl.semaphore_wait(barrier, greeted)
+
+    if opposite:
+
+        @pl.when(zh >= 2)
+        def _():
+            def p_far(dy):
+                to = ((y + dy) % ny) * nzh + zof(2)
+                send(psend.at[to], pb.at[zh, y, zl, co], p1s.at[2, dy], p1r.at[2], at_ka(dy, 2))
+
+            each(0, ny, p_far)
+            for u in range(2):
+                part = vb.at[zh, y, r, u]
+                send(part, part, vgs.at[u], vxr.at[u], at_ka(0, 2))
+
+        @pl.when(zh < 2)
+        def _():
+            way = y // hy
+
+            def p_far(dy):
+                to_y = (y + dy) % ny
+                send(
+                    psend.at[to_y * nzh + zof(2)], prel.at[way, y % hy], p1s.at[2, dy],
+                    prr.at[way], {"ka": to_y * nzh + zof(1 + (nzh - 2) * way)},
+                )
+
+            each(0, ny, p_far)
+
+    for dz in beside[1:]:
+        part = vb.at[zh, y, r]
+        send(part, part, v1s.at[dz], v1r.at[(nzh - dz) % nzh], at_ka(0, dz))
+
+    for dz in reversed(beside):
 
         def p1(dy, dz=dz):
             to = ((y + dy) % ny) * nzh + zof(dz)
@@ -108,14 +147,29 @@
         each(1 if dz == 0 else 0, ny, p1)
 
     load_w.wait()
+    load_q.wait()
     wf[...] = w_v[...].astype(F32)
     for k in range(nka):
         for b in range(nzl):
             ct4[k % nzh, k // nzh, b] = condt[k].reshape(32, nc)
 
-    def first(d):
+    def relay(u):
+        zs, on = zof(nzh - 1 + 2 * u), zof(nzh + 1 - 2 * u)
+        got(vb.at[zs, y, r], v1r.at[(nzh - 1 + 2 * u) % nzh])
+        part = vb.at[zs, y, r, u]
+        send(part, part, vfs.at[0], vxr.at[u], {"ka": y * nzh + on})
+        got(prel.at[u], prr.at[u])
+        send(
+            prel.at[u], pb.at[zs, pl.ds(u * hy, hy), zl, co], pfs.at[0], p1r.at[2],
+            {"ka": y * nzh + on},
+        )
+
+    def first(d, far=False, own=False, relayed=False):
         zs = zof(d)
-        if d:
+        if far:
+            got(vb.at[zs, y, r, 0], vxr.at[0])
+            got(vb.at[zs, y, r, 1], vxr.at[1])
+        elif not (own or relayed):
             got(vb.at[zs, y, r], v1r.at[d])
 
         def v2a(e):
@@ -126,9 +180,18 @@
             part = vb.at[zs, y, r, 1]
             send(part, part, vbs.at[d, e], vbr.at[d], at_row(e))
 
-        each(1, ny, v2a)
-        each(1, nx, v2b)
-        have = ny if d else ny - 1
+        def v_all(e):
+            part = vb.at[zs, y, r]
+            ex, ey = e // ny, e % ny
+            where = {"ka": ((y + ey) % ny) * nzh + zh, "row": (r + ex) % nx}
+            send(part, part, vys.at[ex, ey], vyr.at[ex, ey], where)
+
+        if far:
+            each(1, nx * ny, v_all)
+        else:
+            each(1, ny, v2a)
+            each(1, nx, v2b)
+        have = ny - 1 if own else ny
         if have:
             got(pb.at[zs, 0:have, zl, co], p1r.at[d])
 
@@ -137,6 +200,13 @@
             send(part, part, p2s.at[d, e], p2r.at[d], at_zl(e))
 
         each(1, nzl, p2)
+
+    def second_panels(d):
+        zs = zof(d)
+        if nzl > 1:
+            got(pb.at[zs, :, 0 : nzl - 1, co], p2r.at[d])
+        part = pb.at[zs, :, :, co]
+        send(part, part, pcs.at[d], pcr.at[d], partner)
 
     def second(d):
         zs = zof(d)
@@ -156,18 +226,18 @@
             send(part, part, vds.at[d, e], vdr.at[d], at_ka(e, 0))
 
         each(1, ny, v3b)
-        if nzl > 1:
-            got(pb.at[zs, :, 0 : nzl - 1, co], p2r.at[d])
-        part = pb.at[zs, :, :, co]
-        send(part, part, pcs.at[d], pcr.at[d], partner)
-
-    def third(d):
+        second_panels(d)
+
+    def third(d, far=False):
         zs = zof(d)
         got(pb.at[zs, :, :, co], pcr.at[d])
-        if nx > 1:
-            got(vb.at[zs, :, 0 : nx - 1, 0], vcr.at[d])
-        if ny > 1:
-            got(vb.at[zs, 0 : ny - 1, :, 1], vdr.at[d])
+        if far:
+            each(1, nx * ny, lambda e: got(vb.at[zs, y, r], vyr.at[e // ny, e % ny]))
+        else:
+            if nx > 1:
+                got(vb.at[zs, :, 0 : nx - 1, 0], vcr.at[d])
+            if ny > 1:
+                got(vb.at[zs, 0 : ny - 1, :, 1], vdr.at[d])
 
         def pair(i, carry):
             panel = pb[zs, i].reshape(rows, nv)
@@ -177,42 +247,78 @@
 
         lax.fori_loop(0, ny, pair, 0)
 
-    if nzh == 4:
-        plan = (
-            (first, 0), (first, 1), (first, 3), (second, 0), (first, 2), (second, 1),
-            (second, 3), (third, 0), (second, 2), (third, 1), (third, 3), (third, 2),
-        )
+    lanes = nnu // 128
+
+    def weigh(e, sources, start=False):
+        zk = zof(e)
+
+        def tile(t, carry):
+            s = pl.ds(pl.multiple_of(t * 8, 8), 8)
+            blocks = [pl.ds(l * 128, 128) for l in range(lanes)]
+            place = [(i, b, l) for i in range(ny) for b in range(nzl) for l in range(lanes)]
+            sums = {
+                (i, b, l): None if start else direct[zk, i, b, s, blocks[l]] for i, b, l in place
+            }
+            for d in sources:
+                z2 = zof(d)
+                for y2 in range(ny):
+                    p = [[pairs[z2, y2, b, s, m] for m in blocks] for b in range(nzl)]
+                    for i in range(ny):
+                        q = q_ref[y2 * nzh + z2, i * nzh + zk]
+                        for l in range(lanes):
+                            w = wf[q, s, blocks[l]]
+                            for b in range(nzl):
+                                term = w * p[b][l]
+                                old = sums[i, b, l]
+                                sums[i, b, l] = term if old is None else old + term
+            for i, b, l in place:
+                direct[zk, i, b, s, blocks[l]] = sums[i, b, l]
+            return carry
+
+        lax.fori_loop(0, 4, tile, 0)
+
+    def weigh_all(sources, start=False):
+        def step(e, carry):
+            weigh(e, sources, start)
+            return carry
+
+        lax.fori_loop(0, nzh, step, 0)
+
+    if opposite:
+        u0 = ((zh + 1) // 2 + 1) % 2
+        u1 = 1 - u0
+        d0, d1 = (nzh - 1 + 2 * u0) % nzh, (nzh - 1 + 2 * u1) % nzh
+        relay(u0)
+        first(d0, relayed=True)
+        first(0, own=True)
+        first(d1)
+        second(d0)
+        second(0)
+        first(2, far=True)
+        second(d1)
+        third(d0)
+        second_panels(2)
+        third(0)
+        weigh_all((d0, 0), start=True)
+        third(d1)
+        third(2, far=True)
+        late = (d1, 2)
     else:
-        plan = [(leg, d) for leg in (first, second, third) for d in near]
-    for leg, d in plan:
-        leg(d)
-
-    lanes = nnu // 128
-
-    def weigh(e):
+        for d in near:
+            first(d, own=d == 0)
+        for d in near:
+            second(d)
+        third(0)
+        weigh_all((0,), start=True)
+        for d in near[1:]:
+            third(d)
+        late = tuple(near[1:])
+
+    def halves(e):
         zk = zof(e)
 
-        def tile(t, carry):
-            s = pl.ds(pl.multiple_of((t // lanes) * 8, 8), 8)
-            l = pl.ds(pl.multiple_of((t % lanes) * 128, 128), 128)
-            sums = [[None] * nzl for _ in range(ny)]
-            for z2 in range(nzh):
-                for y2 in range(ny):
-                    p = [pairs[z2, y2, b, s, l] for b in range(nzl)]
-                    for i in range(ny):
-                        w = wf[q_ref[y2 * nzh + z2, i * nzh + zk], s, l]
-                        for b in range(nzl):
-                            term = w * p[b]
-                            sums[i][b] = term if sums[i][b] is None else sums[i][b] + term
-            for i in range(ny):
-                for b in range(nzl):
-                    direct[i, b, s, l] = sums[i][b]
-            return carry
-
-        lax.fori_loop(0, 4 * lanes, tile, 0)
-
         def half(i, carry):
-            d = direct[i].reshape(rows, nnu).astype(BF16)
+            d = direct[zk, i].reshape(rows, nnu).astype(BF16)
             val = vb[zk, i].reshape(nv, nnu)
             h = lax.dot_general(val, d, NT, preferred_element_type=F32)
             hs[zk, i] = h.astype(BF16).reshape(nzl, 2, 16, rows)
@@ -264,18 +370,18 @@
 
     far = near[::-1]
     for i, e in enumerate(far):
-        weigh(e)
+        if late:
+            weigh(e, late)
+        halves(e)
         if i:
             over_zl(far[i - 1])
-    if nzh > 1:
-        over_ka(far[0])
     over_zl(far[-1])
-    for e in far[1:] if nzh > 1 else far:
+    for e in far:
         over_ka(e)
 
     lane_b = lax.broadcasted_iota(jnp.int32, (16, rows), 1) // 32
     total = jnp.zeros((nzl * 16, nc), F32)
-    for d in near:
+    for d in near[1:] + near[:1]:
         have = ny if d else ny - 1
         zs = zof(d)
         if have:
@@ -294,26 +400,40 @@
         send(xs.at[r], xs.at[r], h5s.at[d], h5r.at[d], at_row(d))
 
     each(1, nx, h5)
+
+    for d in range(nzh):
+        lo = 0 if d else 1
+        if d in beside[1:]:
+            got(vb.at[zh, y, r], v1s.at[d])
+        each(lo, ny, lambda e: got(pb.at[zh, y, zl, co], p1s.at[d, e]))
+        if d == 2 and opposite:
+            each(1, nx * ny, lambda e: got(vb.at[zh, y, r], vys.at[e // ny, e % ny]))
+        else:
+            each(1, ny, lambda e: got(vb.at[zh, y, r, 0], vas.at[d, e]))
+            each(1, nx, lambda e: got(vb.at[zh, y, r, 1], vbs.at[d, e]))
+        each(1, nzl, lambda e: got(pb.at[zh, :, zl, co], p2s.at[d, e]))
+        if d != 2 or not opposite:
+            each(1, nx, lambda e: got(vb.at[zh, :, r, 0], vcs.at[d, e]))
+            each(1, ny, lambda e: got(vb.at[zh, y, :, 1], vds.at[d, e]))
+        got(pb.at[zh, :, :, co], pcs.at[d])
+        got(c1.at[zh], h1s.at[d])
+        each(1, nzl, lambda e: got(zr.at[zh, 0], h2s.at[d, e]))
+        each(lo, ny, lambda e: got(fr.at[zh, y], h3s.at[d, e]))
+    if opposite:
+        got(vb.at[zh, y, r, 0], vfs.at[0])
+        got(prel.at[0], pfs.at[0])
+
+        @pl.when(zh >= 2)
+        def _():
+            for u in range(2):
+                got(vb.at[zh, y, r, u], vgs.at[u])
+
     each(1, nx, lambda d: got(xs.at[r], h5r.at[d]))
     result = xs[0].astype(F32)
     for i in range(1, nx):
         result = result + xs[i].astype(F32)
     out_ref[...] = (result * factor).reshape(out_ref.shape)
 
-    for d in range(nzh):
-        if d:
-            got(vb.at[zh, y, r], v1s.at[d])
-        lo = 0 if d else 1
-        each(lo, ny, lambda e: got(pb.at[zh, y, zl, co], p1s.at[d, e]))
-        each(1, ny, lambda e: got(vb.at[zh, y, r, 0], vas.at[d, e]))
-        each(1, nx, lambda e: got(vb.at[zh, y, r, 1], vbs.at[d, e]))
-        each(1, nzl, lambda e: got(pb.at[zh, :, zl, co], p2s.at[d, e]))
-        each(1, nx, lambda e: got(vb.at[zh, :, r, 0], vcs.at[d, e]))
-        each(1, ny, lambda e: got(vb.at[zh, y, :, 1], vds.at[d, e]))
-        got(pb.at[zh, :, :, co], pcs.at[d])
-        got(c1.at[zh], h1s.at[d])
-        each(1, nzl, lambda e: got(zr.at[zh, 0], h2s.at[d, e]))
-        each(lo, ny, lambda e: got(fr.at[zh, y], h3s.at[d, e]))
     each(1, nx, lambda d: got(xs.at[r], h5s.at[d]))
 
 
@@ -332,9 +452,10 @@
         functools.partial(kernel, sizes, factor),
         name="isdf_direct",
         out_shape=jax.ShapeDtypeStruct((nzl, 16, nc), F32),
-        in_specs=[pl.BlockSpec(memory_space=pltpu.SMEM)] + [any_space] * 4,
+        in_specs=[any_space] * 5,
         out_specs=pl.BlockSpec(memory_space=pltpu.VMEM),
         scratch_shapes=[
+            pltpu.SMEM((nka, nka), jnp.int32),
             vm((nv, nc), BF16),
             vm((nc, mu), BF16),
             vm((nka, 2, 16, nc), BF16),
@@ -342,10 +463,11 @@
             vm((nka, 32, nnu), BF16),
             vm((nka, 32, nnu), F32),
             vm((nka, 16, nv), BF16),
+            vm((2, max(1, ny // 2), 16, nv), BF16),
             vm((nzh, ny, nzl, 2, 16, nv), BF16),
             vm((nzh, ny, nx, 2, 16, nnu), BF16),
             vm((nzh, ny, nzl, 32, nnu), F32),
-            vm((ny, nzl, 32, nnu), F32),
+            vm((nzh, ny, nzl, 32, nnu), F32),
             vm((nzh, ny, nzl, 2, 16, rows), BF16),
             vm((nzh, ny, nzl, 16, rows), BF16),
             vm((nzh, nzl, ny, 16, rows), BF16),
@@ -353,10 +475,10 @@
             vm((nzh, ny, 16, rows), BF16),
             vm((nzh, ny, 16, rows), BF16),
             vm((nx, nzl * 16, nc), BF16),
-            dma(4),
-            dma(nzh, ny), dma(nzh),
+            dma(5),
+            dma(nzh, ny), dma(nzh), dma(2), dma(1),
             dma(nzh, nzl), dma(nzh), dma(nzh), dma(nzh),
-            dma(nzh), dma(nzh),
+            dma(nzh), dma(nzh), dma(2), dma(1), dma(2), dma(nx, ny), dma(nx, ny),
             dma(nzh, ny), dma(nzh), dma(nzh, nx), dma(nzh),
             dma(nzh, nx), dma(nzh), dma(nzh, ny), dma(nzh),
             dma(nzh), dma(nzh), dma(nzh, nzl), dma(nzh),

time: 64.4 us -> 59.8 us (0.929)
  the two profiles are of different devices: /device:TPU:96 before, /device:TPU:32 now
where the time goes in v3:
time: 59.8 us; the launch traced here: 59.6 us
  Pallas kernels  58.2 us (97%)
  local copies, waits for them, and re-layouts  1.38 us (2%)
    pallas_call x1, Pallas kernels, local(): pl.pallas_call(functools.partial(kernel, sizes, factor), name='isdf_direc...  58.2 us
    unnamed x1, local copies, waits for them, and re-layouts  1.38 us

profile of v3, /device:TPU:32, one launch (start us, length us, event | category | flops | bytes accessed | tf_op | source)
XLA Modules:
  0.0 59.6 jit_solution(5680714961897409811)
XLA Ops:
  0.0 58.2 %isdf_direct.1 = f32[4,16,128]{2,1,0:T(8,128)} custom-call(s32[16,16]{1,0:T(8,128)} %q_hbm.1, bf16[4,128,128]{2,1,0:T(8,128)(2,1)} %bitcast.7, bf16[128,512]{1,0:T(8,128)(2,1)} %bitcast.8, bf16[4,2,16,256]{3,2,1,0:T(8,128)(2,1)} %bitcast.9, bf16[16,16,32,256]{3,2,1,0:T(8,128)(2,1)} %bitcast.5), custom_call_target="tpu_custom_call" | custom-call | tf_op jit(solution)/shard_map/isdf_direct/pallas_call | solution.py:451
  58.2 1.4 %copy.7 = f32[1,4,16,128]{3,2,1,0:T(8,128)} copy(f32[1,4,16,128]{3,2,1,0:T(8,128)} %bitcast.6) | data formatting | bytes 65536

commit v4 on v3

--- a/solution.py
+++ b/solution.py
@@ -17,7 +17,7 @@
 
 def kernel(
     sizes, factor, q_hbm, ex_hbm, cond_hbm, val_hbm, w_hbm, out_ref,
-    q_ref, ex_v, cond_v, condt, ct4, w_v, wf, psend, prel, pb, vb, pairs, direct, hs, c1, tsum, zr, us, fr, xs,
+    q_ref, ex_v, cond_v, condt, ct4, w_v, wf, psend, powns, prel, pb, vb, pairs, direct, hs, c1, tsum, zr, us, fr, xs,
     ld, p1s, p1r, prr, pfs, p2s, p2r, pcs, pcr, v1s, v1r, vxr, vfs, vgs, vys, vyr, vas, var, vbs, vbr, vcs, vcr, vds, vdr,
     h1s, h1r, h2s, h2r, h3s, h3r, h5s, h5r,
 ):
@@ -61,7 +61,7 @@
         if hi > lo:
             lax.fori_loop(lo, hi, step, 0)
 
-    load_ex = pltpu.make_async_copy(ex_hbm.at[zl], ex_v, ld.at[0])
+    load_ex = pltpu.make_async_copy(ex_hbm, ex_v, ld.at[0])
     load_cond = pltpu.make_async_copy(cond_hbm, cond_v, ld.at[1])
     load_val = pltpu.make_async_copy(val_hbm.at[r], vb.at[zh, y, r], ld.at[2])
     load_w = pltpu.make_async_copy(w_hbm.at[:, a], w_v, ld.at[3])
@@ -94,11 +94,15 @@
     load_ex.wait()
     half_cond = condt[:, co].reshape(nka * 16, nc)
     psend[...] = (
-        lax.dot_general(half_cond, ex_v[...], NT, preferred_element_type=F32)
+        lax.dot_general(half_cond, ex_v[zl], NT, preferred_element_type=F32)
         .astype(BF16)
         .reshape(psend.shape)
     )
-    pb[zh, y, zl, co] = psend[a]
+    own_cond = jnp.concatenate([condt[i * nzh + zh].reshape(32, nc) for i in range(ny)], axis=0)
+    for b in range(nzl):
+        own = lax.dot_general(own_cond, ex_v[b], NT, preferred_element_type=F32)
+        powns[:, b] = own.astype(BF16).reshape(ny, 2, 16, nv)
+    pb[zh, y] = powns[y]
     load_val.wait()
     greeted = ny * len(beside) + nzl + nx - 2
     if opposite:
@@ -135,7 +139,7 @@
         part = vb.at[zh, y, r]
         send(part, part, v1s.at[dz], v1r.at[(nzh - dz) % nzh], at_ka(0, dz))
 
-    for dz in reversed(beside):
+    for dz in reversed(beside[1:]):
 
         def p1(dy, dz=dz):
             to = ((y + dy) % ny) * nzh + zof(dz)
@@ -144,14 +148,12 @@
                 at_ka(dy, dz),
             )
 
-        each(1 if dz == 0 else 0, ny, p1)
-
-    load_w.wait()
-    load_q.wait()
-    wf[...] = w_v[...].astype(F32)
-    for k in range(nka):
-        for b in range(nzl):
-            ct4[k % nzh, k // nzh, b] = condt[k].reshape(32, nc)
+        each(0, ny, p1)
+
+    def p_own(dy):
+        send(powns.at[(y + dy) % ny], pb.at[zh, y], p1s.at[0, dy], p1r.at[0], at_ka(dy, 0))
+
+    each(1, ny, p_own)
 
     def relay(u):
         zs, on = zof(nzh - 1 + 2 * u), zof(nzh + 1 - 2 * u)
@@ -191,9 +193,9 @@
         else:
             each(1, ny, v2a)
             each(1, nx, v2b)
-        have = ny - 1 if own else ny
-        if have:
-            got(pb.at[zs, 0:have, zl, co], p1r.at[d])
+        if own:
+            return
+        got(pb.at[zs, :, zl, co], p1r.at[d])
 
         def p2(e):
             part = pb.at[zs, :, zl, co]
@@ -208,7 +210,7 @@
         part = pb.at[zs, :, :, co]
         send(part, part, pcs.at[d], pcr.at[d], partner)
 
-    def second(d):
+    def second(d, own=False):
         zs = zof(d)
         if ny > 1:
             got(vb.at[zs, 0 : ny - 1, r, 0], var.at[d])
@@ -226,11 +228,15 @@
             send(part, part, vds.at[d, e], vdr.at[d], at_ka(e, 0))
 
         each(1, ny, v3b)
-        second_panels(d)
-
-    def third(d, far=False):
+        if not own:
+            second_panels(d)
+
+    def third(d, far=False, own=False):
         zs = zof(d)
-        got(pb.at[zs, :, :, co], pcr.at[d])
+        if not own:
+            got(pb.at[zs, :, :, co], pcr.at[d])
+        elif ny > 1:
+            got(pb.at[zs, 0 : ny - 1], p1r.at[0])
         if far:
             each(1, nx * ny, lambda e: got(vb.at[zs, y, r], vyr.at[e // ny, e % ny]))
         else:
@@ -239,13 +245,10 @@
             if ny > 1:
                 got(vb.at[zs, 0 : ny - 1, :, 1], vdr.at[d])
 
-        def pair(i, carry):
+        for i in range(ny):
             panel = pb[zs, i].reshape(rows, nv)
             val = vb[zs, i].reshape(nv, nnu)
             pairs[zs, i] = jnp.dot(panel, val, preferred_element_type=F32).reshape(nzl, 32, nnu)
-            return carry
-
-        lax.fori_loop(0, ny, pair, 0)
 
     lanes = nnu // 128
 
@@ -277,39 +280,49 @@
 
         lax.fori_loop(0, 4, tile, 0)
 
-    def weigh_all(sources, start=False):
+    def weigh_all(sources, lo, hi, start=False):
         def step(e, carry):
             weigh(e, sources, start)
             return carry
 
-        lax.fori_loop(0, nzh, step, 0)
+        lax.fori_loop(lo, hi, step, 0)
+
+    first(0, own=True)
+    load_w.wait()
+    load_q.wait()
+    wf[...] = w_v[...].astype(F32)
+    for k in range(nka):
+        for b in range(nzl):
+            ct4[k % nzh, k // nzh, b] = condt[k].reshape(32, nc)
 
     if opposite:
         u0 = ((zh + 1) // 2 + 1) % 2
         u1 = 1 - u0
         d0, d1 = (nzh - 1 + 2 * u0) % nzh, (nzh - 1 + 2 * u1) % nzh
+        second(0, own=True)
         relay(u0)
         first(d0, relayed=True)
-        first(0, own=True)
         first(d1)
+        third(0, own=True)
+        weigh_all((0,), 0, nzh, True)
         second(d0)
-        second(0)
         first(2, far=True)
         second(d1)
         third(d0)
+        before = nzh * (1 - zh // 2)
+        weigh_all((d0,), 0, before)
         second_panels(2)
-        third(0)
-        weigh_all((d0, 0), start=True)
+        weigh_all((d0,), before, nzh)
         third(d1)
         third(2, far=True)
         late = (d1, 2)
     else:
+        for d in near[1:]:
+            first(d)
         for d in near:
-            first(d, own=d == 0)
-        for d in near:
-            second(d)
-        third(0)
-        weigh_all((0,), start=True)
+            second(d, own=d == 0)
+        third(0, own=True)
+        weigh_all((0,), 0, nzh, True)
         for d in near[1:]:
             third(d)
         late = tuple(near[1:])
@@ -317,14 +330,11 @@
     def halves(e):
         zk = zof(e)
 
-        def half(i, carry):
+        for i in range(ny):
             d = direct[zk, i].reshape(rows, nnu).astype(BF16)
             val = vb[zk, i].reshape(nv, nnu)
             h = lax.dot_general(val, d, NT, preferred_element_type=F32)
             hs[zk, i] = h.astype(BF16).reshape(nzl, 2, 16, rows)
-            return carry
-
-        lax.fori_loop(0, ny, half, 0)
         send(hs.at[zk, :, :, 1 - co], c1.at[zk], h1s.at[e], h1r.at[e], partner)
 
     def over_zl(e):
@@ -402,23 +412,25 @@
     each(1, nx, h5)
 
     for d in range(nzh):
-        lo = 0 if d else 1
         if d in beside[1:]:
             got(vb.at[zh, y, r], v1s.at[d])
-        each(lo, ny, lambda e: got(pb.at[zh, y, zl, co], p1s.at[d, e]))
+        if d == 0:
+            each(1, ny, lambda e: got(pb.at[zh, y], p1s.at[d, e]))
+        else:
+            each(0, ny, lambda e: got(pb.at[zh, y, zl, co], p1s.at[d, e]))
+            each(1, nzl, lambda e: got(pb.at[zh, :, zl, co], p2s.at[d, e]))
+            got(pb.at[zh, :, :, co], pcs.at[d])
         if d == 2 and opposite:
             each(1, nx * ny, lambda e: got(vb.at[zh, y, r], vys.at[e // ny, e % ny]))
         else:
             each(1, ny, lambda e: got(vb.at[zh, y, r, 0], vas.at[d, e]))
             each(1, nx, lambda e: got(vb.at[zh, y, r, 1], vbs.at[d, e]))
-        each(1, nzl, lambda e: got(pb.at[zh, :, zl, co], p2s.at[d, e]))
         if d != 2 or not opposite:
             each(1, nx, lambda e: got(vb.at[zh, :, r, 0], vcs.at[d, e]))
             each(1, ny, lambda e: got(vb.at[zh, y, :, 1], vds.at[d, e]))
-        got(pb.at[zh, :, :, co], pcs.at[d])
         got(c1.at[zh], h1s.at[d])
         each(1, nzl, lambda e: got(zr.at[zh, 0], h2s.at[d, e]))
-        each(lo, ny, lambda e: got(fr.at[zh, y], h3s.at[d, e]))
+        each(0 if d else 1, ny, lambda e: got(fr.at[zh, y], h3s.at[d, e]))
     if opposite:
         got(vb.at[zh, y, r, 0], vfs.at[0])
         got(prel.at[0], pfs.at[0])
@@ -456,13 +468,14 @@
         out_specs=pl.BlockSpec(memory_space=pltpu.VMEM),
         scratch_shapes=[
             pltpu.SMEM((nka, nka), jnp.int32),
-            vm((nv, nc), BF16),
+            vm((nzl, nv, nc), BF16),
             vm((nc, mu), BF16),
             vm((nka, 2, 16, nc), BF16),
             vm((nzh, ny, nzl, 32, nc), BF16),
             vm((nka, 32, nnu), BF16),
             vm((nka, 32, nnu), F32),
             vm((nka, 16, nv), BF16),
+            vm((ny, nzl, 2, 16, nv), BF16),
             vm((2, max(1, ny // 2), 16, nv), BF16),
             vm((nzh, ny, nzl, 2, 16, nv), BF16),
             vm((nzh, ny, nx, 2, 16, nnu), BF16),

time: 59.8 us -> 57.1 us (0.955)
  Pallas kernels: 58.2 us -> 55.5 us
    pallas_call x1, Pallas kernels: 58.2 us -> 55.5 us  [local(): pl.pallas_call(functools.partial(kernel, sizes, factor), name='isdf_direc...]
where the time goes in v4:
time: 57.1 us; the launch traced here: 56.9 us
  Pallas kernels  55.5 us (97%)
  local copies, waits for them, and re-layouts  1.38 us (2%)
    pallas_call x1, Pallas kernels, local(): pl.pallas_call(functools.partial(kernel, sizes, factor), name='isdf_direc...  55.5 us
    unnamed x1, local copies, waits for them, and re-layouts  1.38 us

profile of v4, /device:TPU:32, one launch (start us, length us, event | category | flops | bytes accessed | tf_op | source)
XLA Modules:
  0.0 56.9 jit_solution(3434702102170620669)
XLA Ops:
  0.0 55.5 %isdf_direct.1 = f32[4,16,128]{2,1,0:T(8,128)} custom-call(s32[16,16]{1,0:T(8,128)} %q_hbm.1, bf16[4,128,128]{2,1,0:T(8,128)(2,1)} %bitcast.7, bf16[128,512]{1,0:T(8,128)(2,1)} %bitcast.8, bf16[4,2,16,256]{3,2,1,0:T(8,128)(2,1)} %bitcast.9, bf16[16,16,32,256]{3,2,1,0:T(8,128)(2,1)} %bitcast.5), custom_call_target="tpu_custom_call" | custom-call | tf_op jit(solution)/shard_map/isdf_direct/pallas_call | solution.py:463
  55.5 1.4 %copy.7 = f32[1,4,16,128]{3,2,1,0:T(8,128)} copy(f32[1,4,16,128]{3,2,1,0:T(8,128)} %bitcast.6) | data formatting | bytes 65536

commit v5 on v4

--- a/solution.py
+++ b/solution.py
@@ -115,7 +115,7 @@
         def _():
             def p_far(dy):
                 to = ((y + dy) % ny) * nzh + zof(2)
-                send(psend.at[to], pb.at[zh, y, zl, co], p1s.at[2, dy], p1r.at[2], at_ka(dy, 2))
+                send(psend.at[to], pb.at[zh, y, zl, co], p1s.at[2], p1r.at[2], at_ka(dy, 2))
 
             each(0, ny, p_far)
             for u in range(2):
@@ -129,7 +129,7 @@
             def p_far(dy):
                 to_y = (y + dy) % ny
                 send(
-                    psend.at[to_y * nzh + zof(2)], prel.at[way, y % hy], p1s.at[2, dy],
+                    psend.at[to_y * nzh + zof(2)], prel.at[way, y % hy], p1s.at[2],
                     prr.at[way], {"ka": to_y * nzh + zof(1 + (nzh - 2) * way)},
                 )
 
@@ -144,14 +144,14 @@
         def p1(dy, dz=dz):
             to = ((y + dy) % ny) * nzh + zof(dz)
             send(
-                psend.at[to], pb.at[zh, y, zl, co], p1s.at[dz, dy], p1r.at[(nzh - dz) % nzh],
+                psend.at[to], pb.at[zh, y, zl, co], p1s.at[dz], p1r.at[(nzh - dz) % nzh],
                 at_ka(dy, dz),
             )
 
         each(0, ny, p1)
 
     def p_own(dy):
-        send(powns.at[(y + dy) % ny], pb.at[zh, y], p1s.at[0, dy], p1r.at[0], at_ka(dy, 0))
+        send(powns.at[(y + dy) % ny], pb.at[zh, y], p1s.at[0], p1r.at[0], at_ka(dy, 0))
 
     each(1, ny, p_own)
 
@@ -176,17 +176,17 @@
 
         def v2a(e):
             part = vb.at[zs, y, r, 0]
-            send(part, part, vas.at[d, e], var.at[d], at_ka(e, 0))
+            send(part, part, vas.at[d], var.at[d], at_ka(e, 0))
 
         def v2b(e):
             part = vb.at[zs, y, r, 1]
-            send(part, part, vbs.at[d, e], vbr.at[d], at_row(e))
+            send(part, part, vbs.at[d], vbr.at[d], at_row(e))
 
         def v_all(e):
             part = vb.at[zs, y, r]
             ex, ey = e // ny, e % ny
             where = {"ka": ((y + ey) % ny) * nzh + zh, "row": (r + ex) % nx}
-            send(part, part, vys.at[ex, ey], vyr.at[ex, ey], where)
+            send(part, part, vys.at[ex], vyr.at[ex], where)
 
         if far:
             each(1, nx * ny, v_all)
@@ -199,7 +199,7 @@
 
         def p2(e):
             part = pb.at[zs, :, zl, co]
-            send(part, part, p2s.at[d, e], p2r.at[d], at_zl(e))
+            send(part, part, p2s.at[d], p2r.at[d], at_zl(e))
 
         each(1, nzl, p2)
 
@@ -217,7 +217,7 @@
 
         def v3a(e):
             part = vb.at[zs, :, r, 0]
-            send(part, part, vcs.at[d, e], vcr.at[d], at_row(e))
+            send(part, part, vcs.at[d], vcr.at[d], at_row(e))
 
         each(1, nx, v3a)
         if nx > 1:
@@ -225,7 +225,7 @@
 
         def v3b(e):
             part = vb.at[zs, y, :, 1]
-            send(part, part, vds.at[d, e], vdr.at[d], at_ka(e, 0))
+            send(part, part, vds.at[d], vdr.at[d], at_ka(e, 0))
 
         each(1, ny, v3b)
         if not own:
@@ -238,7 +238,9 @@
         elif ny > 1:
             got(pb.at[zs, 0 : ny - 1], p1r.at[0])
         if far:
-            each(1, nx * ny, lambda e: got(vb.at[zs, y, r], vyr.at[e // ny, e % ny]))
+            if ny > 1:
+                got(vb.at[zs, 0 : ny - 1, r], vyr.at[0])
+            each(1, nx, lambda e: got(vb.at[zs, :, r], vyr.at[e]))
         else:
             if nx > 1:
                 got(vb.at[zs, :, 0 : nx - 1, 0], vcr.at[d])
@@ -349,7 +351,7 @@
 
         def h2(d):
             send(
-                tsum.at[zk, (zl + d) % nzl], zr.at[zk, d], h2s.at[e, d], h2r.at[e], at_zl(d)
+                tsum.at[zk, (zl + d) % nzl], zr.at[zk, d], h2s.at[e], h2r.at[e], at_zl(d)
             )
 
         each(1, nzl, h2)
@@ -370,7 +372,7 @@
 
         def h3(dy):
             send(
-                us.at[zk, (y + dy) % ny], fr.at[zh, y], h3s.at[e, dy], h3r.at[(nzh - e) % nzh],
+                us.at[zk, (y + dy) % ny], fr.at[zh, y], h3s.at[e], h3r.at[(nzh - e) % nzh],
                 at_ka(dy, e),
             )
 
@@ -407,30 +409,36 @@
     xs[r] = total.astype(BF16)
 
     def h5(d):
-        send(xs.at[r], xs.at[r], h5s.at[d], h5r.at[d], at_row(d))
+        send(xs.at[r], xs.at[r], h5s.at[0], h5r.at[0], at_row(d))
 
     each(1, nx, h5)
 
     for d in range(nzh):
         if d in beside[1:]:
             got(vb.at[zh, y, r], v1s.at[d])
-        if d == 0:
-            each(1, ny, lambda e: got(pb.at[zh, y], p1s.at[d, e]))
+        if d:
+            got(pb.at[zh, :, zl, co], p1s.at[d])
+            got(pb.at[zh, :, :, co], pcs.at[d])
+            if nzl > 1:
+                got(pb.at[zh, :, 0 : nzl - 1, co], p2s.at[d])
+        elif ny > 1:
+            got(pb.at[zh, 0 : ny - 1], p1s.at[0])
+        if d == 2 and opposite:
+            if ny > 1:
+                got(vb.at[zh, 0 : ny - 1, r], vys.at[0])
+            each(1, nx, lambda e: got(vb.at[zh, :, r], vys.at[e]))
         else:
-            each(0, ny, lambda e: got(pb.at[zh, y, zl, co], p1s.at[d, e]))
-            each(1, nzl, lambda e: got(pb.at[zh, :, zl, co], p2s.at[d, e]))
-            got(pb.at[zh, :, :, co], pcs.at[d])
-        if d == 2 and opposite:
-            each(1, nx * ny, lambda e: got(vb.at[zh, y, r], vys.at[e // ny, e % ny]))
-        else:
-            each(1, ny, lambda e: got(vb.at[zh, y, r, 0], vas.at[d, e]))
-            each(1, nx, lambda e: got(vb.at[zh, y, r, 1], vbs.at[d, e]))
-        if d != 2 or not opposite:
-            each(1, nx, lambda e: got(vb.at[zh, :, r, 0], vcs.at[d, e]))
-            each(1, ny, lambda e: got(vb.at[zh, y, :, 1], vds.at[d, e]))
+            if ny > 1:
+                got(vb.at[zh, 0 : ny - 1, r, 0], vas.at[d])
+                got(vb.at[zh, 0 : ny - 1, :, 1], vds.at[d])
+            if nx > 1:
+                got(vb.at[zh, y, 0 : nx - 1, 1], vbs.at[d])
+                got(vb.at[zh, :, 0 : nx - 1, 0], vcs.at[d])
         got(c1.at[zh], h1s.at[d])
-        each(1, nzl, lambda e: got(zr.at[zh, 0], h2s.at[d, e]))
-        each(0 if d else 1, ny, lambda e: got(fr.at[zh, y], h3s.at[d, e]))
+        if nzl > 1:
+            got(zr.at[zh, 0 : nzl - 1], h2s.at[d])
+        if d or ny > 1:
+            got(fr.at[zh, 0 : ny if d else ny - 1], h3s.at[d])
     if opposite:
         got(vb.at[zh, y, r, 0], vfs.at[0])
         got(prel.at[0], pfs.at[0])
@@ -440,13 +448,15 @@
             for u in range(2):
                 got(vb.at[zh, y, r, u], vgs.at[u])
 
-    each(1, nx, lambda d: got(xs.at[r], h5r.at[d]))
+    if nx > 1:
+        got(xs.at[0 : nx - 1], h5r.at[0])
     result = xs[0].astype(F32)
     for i in range(1, nx):
         result = result + xs[i].astype(F32)
     out_ref[...] = (result * factor).reshape(out_ref.shape)
 
-    each(1, nx, lambda d: got(xs.at[r], h5s.at[d]))
+    if nx > 1:
+        got(xs.at[0 : nx - 1], h5s.at[0])
 
 
 def local(sizes, factor, exciton, orb_cond, orb_val, screened, q_table):
@@ -489,13 +499,13 @@
             vm((nzh, ny, 16, rows), BF16),
             vm((nx, nzl * 16, nc), BF16),
             dma(5),
-            dma(nzh, ny), dma(nzh), dma(2), dma(1),
-            dma(nzh, nzl), dma(nzh), dma(nzh), dma(nzh),
-            dma(nzh), dma(nzh), dma(2), dma(1), dma(2), dma(nx, ny), dma(nx, ny),
-            dma(nzh, ny), dma(nzh), dma(nzh, nx), dma(nzh),
-            dma(nzh, nx), dma(nzh), dma(nzh, ny), dma(nzh),
-            dma(nzh), dma(nzh), dma(nzh, nzl), dma(nzh),
-            dma(nzh, ny), dma(nzh), dma(nx), dma(nx),
+            dma(nzh), dma(nzh), dma(2), dma(1),
+            dma(nzh), dma(nzh), dma(nzh), dma(nzh),
+            dma(nzh), dma(nzh), dma(2), dma(1), dma(2), dma(nx), dma(nx),
+            dma(nzh), dma(nzh), dma(nzh), dma(nzh),
+            dma(nzh), dma(nzh), dma(nzh), dma(nzh),
+            dma(nzh), dma(nzh), dma(nzh), dma(nzh),
+            dma(nzh), dma(nzh), dma(1), dma(1),
         ],
         compiler_params=pltpu.CompilerParams(
             collective_id=0, has_side_effects=True, vmem_limit_bytes=56 * 1024 * 1024

time: 57.1 us -> 55 us (0.963)
  Pallas kernels: 55.5 us -> 53.4 us
    pallas_call x1, Pallas kernels: 55.5 us -> 53.4 us  [local(): pl.pallas_call(functools.partial(kernel, sizes, factor), name='isdf_direc...]
where the time goes in v5:
time: 55 us; the launch traced here: 54.8 us
  Pallas kernels  53.4 us (97%)
  local copies, waits for them, and re-layouts  1.38 us (3%)
    pallas_call x1, Pallas kernels, local(): pl.pallas_call(functools.partial(kernel, sizes, factor), name='isdf_direc...  53.4 us
    unnamed x1, local copies, waits for them, and re-layouts  1.38 us

profile of v5, /device:TPU:32, one launch (start us, length us, event | category | flops | bytes accessed | tf_op | source)
XLA Modules:
  0.0 54.8 jit_solution(3692805008571537413)
XLA Ops:
  0.0 53.4 %isdf_direct.1 = f32[4,16,128]{2,1,0:T(8,128)} custom-call(s32[16,16]{1,0:T(8,128)} %q_hbm.1, bf16[4,128,128]{2,1,0:T(8,128)(2,1)} %bitcast.7, bf16[128,512]{1,0:T(8,128)(2,1)} %bitcast.8, bf16[4,2,16,256]{3,2,1,0:T(8,128)(2,1)} %bitcast.9, bf16[16,16,32,256]{3,2,1,0:T(8,128)(2,1)} %bitcast.5), custom_call_target="tpu_custom_call" | custom-call | tf_op jit(solution)/shard_map/isdf_direct/pallas_call | solution.py:473
  53.4 1.4 %copy.7 = f32[1,4,16,128]{3,2,1,0:T(8,128)} copy(f32[1,4,16,128]{3,2,1,0:T(8,128)} %bitcast.6) | data formatting | bytes 65536

commit v6 on v5

--- a/solution.py
+++ b/solution.py
@@ -115,12 +115,12 @@
         def _():
             def p_far(dy):
                 to = ((y + dy) % ny) * nzh + zof(2)
-                send(psend.at[to], pb.at[zh, y, zl, co], p1s.at[2], p1r.at[2], at_ka(dy, 2))
+                send(psend.at[to], pb.at[zh, y, zl, co], p1s.at[0], p1r.at[2], at_ka(dy, 2))
 
             each(0, ny, p_far)
             for u in range(2):
                 part = vb.at[zh, y, r, u]
-                send(part, part, vgs.at[u], vxr.at[u], at_ka(0, 2))
+                send(part, part, vgs.at[0], vxr.at[u], at_ka(0, 2))
 
         @pl.when(zh < 2)
         def _():
@@ -129,7 +129,7 @@
             def p_far(dy):
                 to_y = (y + dy) % ny
                 send(
-                    psend.at[to_y * nzh + zof(2)], prel.at[way, y % hy], p1s.at[2],
+                    psend.at[to_y * nzh + zof(2)], prel.at[way, y % hy], p1s.at[0],
                     prr.at[way], {"ka": to_y * nzh + zof(1 + (nzh - 2) * way)},
                 )
 
@@ -137,21 +137,21 @@
 
     for dz in beside[1:]:
         part = vb.at[zh, y, r]
-        send(part, part, v1s.at[dz], v1r.at[(nzh - dz) % nzh], at_ka(0, dz))
+        send(part, part, v1s.at[0], v1r.at[(nzh - dz) % nzh], at_ka(0, dz))
 
     for dz in reversed(beside[1:]):
 
         def p1(dy, dz=dz):
             to = ((y + dy) % ny) * nzh + zof(dz)
             send(
-                psend.at[to], pb.at[zh, y, zl, co], p1s.at[dz], p1r.at[(nzh - dz) % nzh],
+                psend.at[to], pb.at[zh, y, zl, co], p1s.at[0], p1r.at[(nzh - dz) % nzh],
                 at_ka(dy, dz),
             )
 
         each(0, ny, p1)
 
     def p_own(dy):
-        send(powns.at[(y + dy) % ny], pb.at[zh, y], p1s.at[0], p1r.at[0], at_ka(dy, 0))
+        send(powns.at[(y + dy) % ny], pb.at[zh, y], p1s.at[1], p1r.at[0], at_ka(dy, 0))
 
     each(1, ny, p_own)
 
@@ -176,20 +176,21 @@
 
         def v2a(e):
             part = vb.at[zs, y, r, 0]
-            send(part, part, vas.at[d], var.at[d], at_ka(e, 0))
+            send(part, part, vas.at[0], var.at[d], at_ka(e, 0))
 
         def v2b(e):
             part = vb.at[zs, y, r, 1]
-            send(part, part, vbs.at[d], vbr.at[d], at_row(e))
-
-        def v_all(e):
+            send(part, part, vbs.at[0], vbr.at[d], at_row(e))
+
+        def v_all(e, other):
             part = vb.at[zs, y, r]
             ex, ey = e // ny, e % ny
             where = {"ka": ((y + ey) % ny) * nzh + zh, "row": (r + ex) % nx}
-            send(part, part, vys.at[ex], vyr.at[ex], where)
+            send(part, part, vys.at[other], vyr.at[other], where)
 
         if far:
-            each(1, nx * ny, v_all)
+            each(1, ny, lambda e: v_all(e, 0))
+            each(ny, nx * ny, lambda e: v_all(e, 1))
         else:
             each(1, ny, v2a)
             each(1, nx, v2b)
@@ -199,7 +200,7 @@
 
         def p2(e):
             part = pb.at[zs, :, zl, co]
-            send(part, part, p2s.at[d], p2r.at[d], at_zl(e))
+            send(part, part, p2s.at[0], p2r.at[d], at_zl(e))
 
         each(1, nzl, p2)
 
@@ -208,7 +209,7 @@
         if nzl > 1:
             got(pb.at[zs, :, 0 : nzl - 1, co], p2r.at[d])
         part = pb.at[zs, :, :, co]
-        send(part, part, pcs.at[d], pcr.at[d], partner)
+        send(part, part, pcs.at[0], pcr.at[d], partner)
 
     def second(d, own=False):
         zs = zof(d)
@@ -217,7 +218,7 @@
 
         def v3a(e):
             part = vb.at[zs, :, r, 0]
-            send(part, part, vcs.at[d], vcr.at[d], at_row(e))
+            send(part, part, vcs.at[0], vcr.at[d], at_row(e))
 
         each(1, nx, v3a)
         if nx > 1:
@@ -225,7 +226,7 @@
 
         def v3b(e):
             part = vb.at[zs, y, :, 1]
-            send(part, part, vds.at[d], vdr.at[d], at_ka(e, 0))
+            send(part, part, vds.at[0], vdr.at[d], at_ka(e, 0))
 
         each(1, ny, v3b)
         if not own:
@@ -240,7 +241,8 @@
         if far:
             if ny > 1:
                 got(vb.at[zs, 0 : ny - 1, r], vyr.at[0])
-            each(1, nx, lambda e: got(vb.at[zs, :, r], vyr.at[e]))
+            if nx > 1:
+                got(vb.at[0 : nx - 1, :, r], vyr.at[1])
         else:
             if nx > 1:
                 got(vb.at[zs, :, 0 : nx - 1, 0], vcr.at[d])
@@ -337,7 +339,7 @@
             val = vb[zk, i].reshape(nv, nnu)
             h = lax.dot_general(val, d, NT, preferred_element_type=F32)
             hs[zk, i] = h.astype(BF16).reshape(nzl, 2, 16, rows)
-        send(hs.at[zk, :, :, 1 - co], c1.at[zk], h1s.at[e], h1r.at[e], partner)
+        send(hs.at[zk, :, :, 1 - co], c1.at[zk], h1s.at[0], h1r.at[e], partner)
 
     def over_zl(e):
         zk = zof(e)
@@ -351,7 +353,7 @@
 
         def h2(d):
             send(
-                tsum.at[zk, (zl + d) % nzl], zr.at[zk, d], h2s.at[e], h2r.at[e], at_zl(d)
+                tsum.at[zk, (zl + d) % nzl], zr.at[zk, d], h2s.at[0], h2r.at[e], at_zl(d)
             )
 
         each(1, nzl, h2)
@@ -372,7 +374,7 @@
 
         def h3(dy):
             send(
-                us.at[zk, (y + dy) % ny], fr.at[zh, y], h3s.at[e], h3r.at[(nzh - e) % nzh],
+                us.at[zk, (y + dy) % ny], fr.at[zh, y], h3s.at[0 if e else 1], h3r.at[(nzh - e) % nzh],
                 at_ka(dy, e),
             )
 
@@ -413,40 +415,36 @@
 
     each(1, nx, h5)
 
-    for d in range(nzh):
-        if d in beside[1:]:
-            got(vb.at[zh, y, r], v1s.at[d])
-        if d:
-            got(pb.at[zh, :, zl, co], p1s.at[d])
-            got(pb.at[zh, :, :, co], pcs.at[d])
-            if nzl > 1:
-                got(pb.at[zh, :, 0 : nzl - 1, co], p2s.at[d])
-        elif ny > 1:
-            got(pb.at[zh, 0 : ny - 1], p1s.at[0])
-        if d == 2 and opposite:
-            if ny > 1:
-                got(vb.at[zh, 0 : ny - 1, r], vys.at[0])
-            each(1, nx, lambda e: got(vb.at[zh, :, r], vys.at[e]))
-        else:
-            if ny > 1:
-                got(vb.at[zh, 0 : ny - 1, r, 0], vas.at[d])
-                got(vb.at[zh, 0 : ny - 1, :, 1], vds.at[d])
-            if nx > 1:
-                got(vb.at[zh, y, 0 : nx - 1, 1], vbs.at[d])
-                got(vb.at[zh, :, 0 : nx - 1, 0], vcs.at[d])
-        got(c1.at[zh], h1s.at[d])
+    legs = nzh - 1 if opposite else nzh
+    if nzh > 1:
+        got(vb.at[0 : len(beside) - 1, y, r], v1s.at[0])
+        got(pb.at[0 : nzh - 1, :, zl, co], p1s.at[0])
+        got(pb.at[0 : nzh - 1, :, :, co], pcs.at[0])
+        got(fr.at[0 : nzh - 1], h3s.at[0])
         if nzl > 1:
-            got(zr.at[zh, 0 : nzl - 1], h2s.at[d])
-        if d or ny > 1:
-            got(fr.at[zh, 0 : ny if d else ny - 1], h3s.at[d])
+            got(pb.at[0 : nzh - 1, :, 0 : nzl - 1, co], p2s.at[0])
+    if ny > 1:
+        got(pb.at[zh, 0 : ny - 1], p1s.at[1])
+        got(fr.at[zh, 0 : ny - 1], h3s.at[1])
+        got(vb.at[0:legs, 0 : ny - 1, r, 0], vas.at[0])
+        got(vb.at[0:legs, 0 : ny - 1, :, 1], vds.at[0])
+    if nx > 1:
+        got(vb.at[0:legs, y, 0 : nx - 1, 1], vbs.at[0])
+        got(vb.at[0:legs, :, 0 : nx - 1, 0], vcs.at[0])
+    got(c1, h1s.at[0])
+    if nzl > 1:
+        got(zr.at[:, 0 : nzl - 1], h2s.at[0])
     if opposite:
+        if ny > 1:
+            got(vb.at[zh, 0 : ny - 1, r], vys.at[0])
+        if nx > 1:
+            got(vb.at[0 : nx - 1, :, r], vys.at[1])
         got(vb.at[zh, y, r, 0], vfs.at[0])
         got(prel.at[0], pfs.at[0])
 
         @pl.when(zh >= 2)
         def _():
-            for u in range(2):
-                got(vb.at[zh, y, r, u], vgs.at[u])
+            got(vb.at[zh, y, r], vgs.at[0])
 
     if nx > 1:
         got(xs.at[0 : nx - 1], h5r.at[0])
@@ -499,13 +497,13 @@
             vm((nzh, ny, 16, rows), BF16),
             vm((nx, nzl * 16, nc), BF16),
             dma(5),
-            dma(nzh), dma(nzh), dma(2), dma(1),
-            dma(nzh), dma(nzh), dma(nzh), dma(nzh),
-            dma(nzh), dma(nzh), dma(2), dma(1), dma(2), dma(nx), dma(nx),
-            dma(nzh), dma(nzh), dma(nzh), dma(nzh),
-            dma(nzh), dma(nzh), dma(nzh), dma(nzh),
-            dma(nzh), dma(nzh), dma(nzh), dma(nzh),
-            dma(nzh), dma(nzh), dma(1), dma(1),
+            dma(2), dma(nzh), dma(2), dma(1),
+            dma(1), dma(nzh), dma(1), dma(nzh),
+            dma(1), dma(nzh), dma(2), dma(1), dma(1), dma(2), dma(2),
+            dma(1), dma(nzh), dma(1), dma(nzh),
+            dma(1), dma(nzh), dma(1), dma(nzh),
+            dma(1), dma(nzh), dma(1), dma(nzh),
+            dma(2), dma(nzh), dma(1), dma(1),
         ],
         compiler_params=pltpu.CompilerParams(
             collective_id=0, has_side_effects=True, vmem_limit_bytes=56 * 1024 * 1024

time: 55 us -> 54.7 us (level)
  no operation moved by 1% of the time
where the time goes in v6:
time: 54.7 us; the launch traced here: 54.5 us
  Pallas kernels  53.1 us (97%)
  local copies, waits for them, and re-layouts  1.38 us (3%)
    pallas_call x1, Pallas kernels, local(): pl.pallas_call(functools.partial(kernel, sizes, factor), name='isdf_direc...  53.1 us
    unnamed x1, local copies, waits for them, and re-layouts  1.38 us

profile of v6, /device:TPU:32, one launch (start us, length us, event | category | flops | bytes accessed | tf_op | source)
XLA Modules:
  0.0 54.5 jit_solution(13931751401265081423)
XLA Ops:
  0.0 53.1 %isdf_direct.1 = f32[4,16,128]{2,1,0:T(8,128)} custom-call(s32[16,16]{1,0:T(8,128)} %q_hbm.1, bf16[4,128,128]{2,1,0:T(8,128)(2,1)} %bitcast.7, bf16[128,512]{1,0:T(8,128)(2,1)} %bitcast.8, bf16[4,2,16,256]{3,2,1,0:T(8,128)(2,1)} %bitcast.9, bf16[16,16,32,256]{3,2,1,0:T(8,128)(2,1)} %bitcast.5), custom_call_target="tpu_custom_call" | custom-call | tf_op jit(solution)/shard_map/isdf_direct/pallas_call | solution.py:471
  53.1 1.4 %copy.7 = f32[1,4,16,128]{3,2,1,0:T(8,128)} copy(f32[1,4,16,128]{3,2,1,0:T(8,128)} %bitcast.6) | data formatting | bytes 65536

commit v7 on v6

--- a/solution.py
+++ b/solution.py
@@ -41,6 +41,9 @@
 
     def at_row(d):
         return {"row": (r + d) % nx}
+
+    def leg_of(d):
+        return d - d // 2 if opposite else d
 
     def zof(d):
         return (zh + d) % nzh
@@ -137,7 +140,7 @@
 
     for dz in beside[1:]:
         part = vb.at[zh, y, r]
-        send(part, part, v1s.at[0], v1r.at[(nzh - dz) % nzh], at_ka(0, dz))
+        send(part, part, v1s.at[0], v1r.at[(nzh - dz) % nzh // 2], at_ka(0, dz))
 
     for dz in reversed(beside[1:]):
 
@@ -157,7 +160,7 @@
 
     def relay(u):
         zs, on = zof(nzh - 1 + 2 * u), zof(nzh + 1 - 2 * u)
-        got(vb.at[zs, y, r], v1r.at[(nzh - 1 + 2 * u) % nzh])
+        got(vb.at[zs, y, r], v1r.at[(nzh - 1 + 2 * u) % nzh // 2])
         part = vb.at[zs, y, r, u]
         send(part, part, vfs.at[0], vxr.at[u], {"ka": y * nzh + on})
         got(prel.at[u], prr.at[u])
@@ -172,15 +175,15 @@
             got(vb.at[zs, y, r, 0], vxr.at[0])
             got(vb.at[zs, y, r, 1], vxr.at[1])
         elif not (own or relayed):
-            got(vb.at[zs, y, r], v1r.at[d])
+            got(vb.at[zs, y, r], v1r.at[d // 2])
 
         def v2a(e):
             part = vb.at[zs, y, r, 0]
-            send(part, part, vas.at[0], var.at[d], at_ka(e, 0))
+            send(part, part, vas.at[0], var.at[leg_of(d)], at_ka(e, 0))
 
         def v2b(e):
             part = vb.at[zs, y, r, 1]
-            send(part, part, vbs.at[0], vbr.at[d], at_row(e))
+            send(part, part, vbs.at[0], vbr.at[leg_of(d)], at_row(e))
 
         def v_all(e, other):
             part = vb.at[zs, y, r]
@@ -200,33 +203,33 @@
 
         def p2(e):
             part = pb.at[zs, :, zl, co]
-            send(part, part, p2s.at[0], p2r.at[d], at_zl(e))
+            send(part, part, p2s.at[0], p2r.at[d - 1], at_zl(e))
 
         each(1, nzl, p2)
 
     def second_panels(d):
         zs = zof(d)
         if nzl > 1:
-            got(pb.at[zs, :, 0 : nzl - 1, co], p2r.at[d])
+            got(pb.at[zs, :, 0 : nzl - 1, co], p2r.at[d - 1])
         part = pb.at[zs, :, :, co]
-        send(part, part, pcs.at[0], pcr.at[d], partner)
+        send(part, part, pcs.at[0], pcr.at[d - 1], partner)
 
     def second(d, own=False):
         zs = zof(d)
         if ny > 1:
-            got(vb.at[zs, 0 : ny - 1, r, 0], var.at[d])
+            got(vb.at[zs, 0 : ny - 1, r, 0], var.at[leg_of(d)])
 
         def v3a(e):
             part = vb.at[zs, :, r, 0]
-            send(part, part, vcs.at[0], vcr.at[d], at_row(e))
+            send(part, part, vcs.at[0], vcr.at[leg_of(d)], at_row(e))
 
         each(1, nx, v3a)
         if nx > 1:
-            got(vb.at[zs, y, 0 : nx - 1, 1], vbr.at[d])
+            got(vb.at[zs, y, 0 : nx - 1, 1], vbr.at[leg_of(d)])
 
         def v3b(e):
             part = vb.at[zs, y, :, 1]
-            send(part, part, vds.at[0], vdr.at[d], at_ka(e, 0))
+            send(part, part, vds.at[0], vdr.at[leg_of(d)], at_ka(e, 0))
 
         each(1, ny, v3b)
         if not own:
@@ -235,7 +238,7 @@
     def third(d, far=False, own=False):
         zs = zof(d)
         if not own:
-            got(pb.at[zs, :, :, co], pcr.at[d])
+            got(pb.at[zs, :, :, co], pcr.at[d - 1])
         elif ny > 1:
             got(pb.at[zs, 0 : ny - 1], p1r.at[0])
         if far:
@@ -245,9 +248,9 @@
                 got(vb.at[0 : nx - 1, :, r], vyr.at[1])
         else:
             if nx > 1:
-                got(vb.at[zs, :, 0 : nx - 1, 0], vcr.at[d])
+                got(vb.at[zs, :, 0 : nx - 1, 0], vcr.at[leg_of(d)])
             if ny > 1:
-                got(vb.at[zs, 0 : ny - 1, :, 1], vdr.at[d])
+                got(vb.at[zs, 0 : ny - 1, :, 1], vdr.at[leg_of(d)])
 
         for i in range(ny):
             panel = pb[zs, i].reshape(rows, nv)
@@ -460,6 +463,7 @@
 def local(sizes, factor, exciton, orb_cond, orb_val, screened, q_table):
     ny, nzh, nx, nzl = sizes
     nka = ny * nzh
+    legs = nzh - 1 if nzh > 2 else nzh
     nc = exciton.shape[-1]
     nv = nzl * 32
     rows = nzl * 32
@@ -498,10 +502,10 @@
             vm((nx, nzl * 16, nc), BF16),
             dma(5),
             dma(2), dma(nzh), dma(2), dma(1),
-            dma(1), dma(nzh), dma(1), dma(nzh),
-            dma(1), dma(nzh), dma(2), dma(1), dma(1), dma(2), dma(2),
-            dma(1), dma(nzh), dma(1), dma(nzh),
-            dma(1), dma(nzh), dma(1), dma(nzh),
+            dma(1), dma(max(1, nzh - 1)), dma(1), dma(max(1, nzh - 1)),
+            dma(1), dma(max(1, nzh // 2)), dma(2), dma(1), dma(1), dma(2), dma(2),
+            dma(1), dma(legs), dma(1), dma(legs),
+            dma(1), dma(legs), dma(1), dma(legs),
             dma(1), dma(nzh), dma(1), dma(nzh),
             dma(2), dma(nzh), dma(1), dma(1),
         ],

time: 54.7 us -> 54.6 us (level)
  no operation moved by 1% of the time
where the time goes in v7:
time: 54.6 us; the launch traced here: 54.4 us
  Pallas kernels  53 us (97%)
  local copies, waits for them, and re-layouts  1.38 us (3%)
    pallas_call x1, Pallas kernels, local(): pl.pallas_call(functools.partial(kernel, sizes, factor), name='isdf_direc...  53 us
    unnamed x1, local copies, waits for them, and re-layouts  1.38 us

profile of v7, /device:TPU:32, one launch (start us, length us, event | category | flops | bytes accessed | tf_op | source)
XLA Modules:
  0.0 54.4 jit_solution(4546592489525690517)
XLA Ops:
  0.0 53.0 %isdf_direct.1 = f32[4,16,128]{2,1,0:T(8,128)} custom-call(s32[16,16]{1,0:T(8,128)} %q_hbm.1, bf16[4,128,128]{2,1,0:T(8,128)(2,1)} %bitcast.7, bf16[128,512]{1,0:T(8,128)(2,1)} %bitcast.8, bf16[4,2,16,256]{3,2,1,0:T(8,128)(2,1)} %bitcast.9, bf16[16,16,32,256]{3,2,1,0:T(8,128)(2,1)} %bitcast.5), custom_call_target="tpu_custom_call" | custom-call | tf_op jit(solution)/shard_map/isdf_direct/pallas_call | solution.py:475
  53.0 1.4 %copy.7 = f32[1,4,16,128]{3,2,1,0:T(8,128)} copy(f32[1,4,16,128]{3,2,1,0:T(8,128)} %bitcast.6) | data formatting | bytes 65536
